TPU v7x, 32 devices: a whole 2x2x4 slice. The times are simulated.
32 devices in a mesh: groups: 2 (over x), tile: 16 (over z, y, core).
Axes of the slice: x: 2, y: 2, z: 4, core: 2. Of those that a mesh axis runs over, the one named last changes fastest.
Arguments:
- reference_feat: float32 [8, 1024, 256], P('groups', 'tile'), parts along dimension 0, may hold values from -32 to 32
- secondary_feat: float32 [4, 4, 1024, 256], P('groups', None, 'tile'), parts along dimension 0, may hold values from -32 to 32
- pair_offsets: int32 [4, 16], P('groups', 'tile'), parts along dimension 0, may hold values from 0 to 63, as said below
- w_query_key: float32 [256, 64], replicated, may hold values from -0.375 to 0.375
- w_value: float32 [256, 64], replicated, may hold values from -0.375 to 0.375
- conv_first: float32 [8, 8, 3, 3, 3], replicated, may hold values from -0.8 to 0.8
- conv_second: float32 [8, 8, 3, 3, 3], replicated, may hold values from -0.4 to 0.4
Outputs:
- disparity: float32 [8, 1024], P('groups', 'tile'), parts along dimension 0
There are 2 independent parts, one for each index of `groups`. A program takes and returns all parts, laid end to end along the dimension named above; an argument that names none is the same for every part. Nothing has to cross between parts.
Inputs may be any that keep to these rules, and one draw needn't show every extreme that they name: `pair_offsets`: in each pair's row some tile holds 63 and the next tile, cyclically, holds 0.
All inputs are finite; a program needn't handle non-finite values.
Results may differ from a plain program's by a relative error of at most 0.0003.
Values sent between devices are 32-bit elements; how exact they have to be, the bound alone decides.
A program may use at most 192 MiB of HBM per device.

v0:
```python
from functools import reduce

import jax
import jax.numpy as jnp
from jax import lax
from jax.sharding import PartitionSpec as P

CORR_GROUPS = 8
DISP = 128
RAD = 3


precise = lax.Precision.HIGHEST


def with_halo(array, sides, width):
    for axis, dim in sides:
        devices, length = (lax.axis_size(axis), array.shape[dim])
        up = [(i, (i + 1) % devices) for i in range(devices - 1)]
        down = [(j, i) for i, j in up]
        last = lax.slice_in_dim(array, length - width, length, axis=dim)
        first = lax.slice_in_dim(array, 0, width, axis=dim)
        before = lax.ppermute(last, axis, up)
        after = lax.ppermute(first, axis, down)
        array = jnp.concatenate([before, array, after], axis=dim)
    return array


def passed_along(value, axis, steps):
    count = lax.axis_size(axis)
    first, last = (max(0, -steps), min(count, count - steps))
    return lax.ppermute(value, axis, [(source, source + steps) for source in range(first, last)])


def window_attention(query_key, value_proj, widened, row_valid, col_valid, channels):
    row_count = query_key.shape[1]
    col_count = query_key.shape[2]
    scores = []
    for row_step in range(3):
        for col_step in range(2 * RAD + 1):
            keys_here = widened[
                :, row_step : row_step + row_count, col_step : col_step + col_count, :channels
            ]
            allowed = (
                row_valid[row_step : row_step + row_count][:, None]
                & col_valid[col_step : col_step + col_count][None, :]
            )
            raw_score = jnp.sum(query_key * keys_here, axis=-1) / channels
            scores.append(jnp.where(allowed[None], raw_score, -1e30))
    row_peak = reduce(jnp.maximum, scores)
    weights = [jnp.exp(score_one - row_peak) for score_one in scores]
    exp_sum = reduce(jnp.add, weights)
    mixed = jnp.zeros(value_proj.shape, jnp.float32)
    position = 0
    for row_step in range(3):
        for col_step in range(2 * RAD + 1):
            vals_here = widened[
                :, row_step : row_step + row_count, col_step : col_step + col_count, channels:
            ]
            mixed = mixed + weights[position][..., None] * vals_here
            position = position + 1
    return value_proj + mixed / exp_sum[..., None]


def neighborhood(images, w_query_key, w_value, tile_id, cycle_size):
    query_key = jnp.einsum("vrxf,fc->vrxc", images, w_query_key, precision=precise)
    value_proj = jnp.einsum("vrxf,fc->vrxc", images, w_value, precision=precise)
    channels = query_key.shape[-1]
    row_count = images.shape[1]
    col_count = images.shape[2]
    joined = jnp.concatenate([query_key, value_proj], axis=-1)
    widened = with_halo(joined, (("tile", 2),), RAD)
    widened = jnp.pad(widened, ((0, 0), (1, 1), (0, 0), (0, 0)))
    row_ids = jnp.arange(row_count + 2)
    col_ids = jnp.arange(col_count + 2 * RAD)
    row_valid = (row_ids >= 1) & (row_ids <= row_count)
    col_valid = ((col_ids >= RAD) | (tile_id > 0)) & (
        (col_ids < col_count + RAD) | (tile_id < cycle_size - 1)
    )
    return window_attention(query_key, value_proj, widened, row_valid, col_valid, channels)


def secondary_window(right_feat):
    next_one = passed_along(right_feat, "tile", -1)
    paired = jnp.concatenate([right_feat, next_one], axis=2)
    moved_pair = passed_along(paired, "tile", -2)
    return jnp.concatenate([paired, moved_pair], axis=2)


def correlate_local(left_feat, window, shift, tile_width):
    row_count = left_feat.shape[0]
    channels = left_feat.shape[2]
    group_size = channels // CORR_GROUPS
    span_len = tile_width + DISP
    picked = lax.dynamic_slice_in_dim(window, shift, span_len, 1)
    left_groups = left_feat.reshape(row_count, tile_width, CORR_GROUPS, group_size)
    right_groups = picked.reshape(row_count, span_len, CORR_GROUPS, group_size)
    products = (
        jnp.einsum("rxgc,rygc->grxy", left_groups, right_groups, precision=precise) / group_size
    )
    flat_prod = products.reshape(CORR_GROUPS, row_count, tile_width * span_len)
    flat_prod = jnp.pad(flat_prod, ((0, 0), (0, 0), (0, tile_width)))
    return flat_prod.reshape(CORR_GROUPS, row_count, tile_width * 0 + tile_width, span_len + 1)[
        ..., :DISP
    ]


def tap_view(plane, row_tap, col_tap, disp_tap, out_cols):
    row_count = plane.shape[0]
    rowed = jnp.pad(plane, ((1, 1), (0, 0), (0, 0)))[
        row_tap : row_tap + row_count, col_tap : col_tap + out_cols, :
    ]
    if disp_tap == 0:
        return jnp.pad(rowed[:, :, :-1], ((0, 0), (0, 0), (1, 0)))
    if disp_tap == 2:
        return jnp.pad(rowed[:, :, 1:], ((0, 0), (0, 0), (0, 1)))
    return rowed


def conv_relu(source, weights, out_cols):
    in_count = source.shape[0]
    total = None
    for in_pos in range(in_count):
        for row_tap in range(3):
            for col_tap in range(3):
                for disp_tap in range(3):
                    view = tap_view(source[in_pos], row_tap, col_tap, disp_tap, out_cols)
                    term = (
                        weights[:, in_pos, row_tap, col_tap, disp_tap][:, None, None, None]
                        * view[None]
                    )
                    total = term if total is None else total + term
    return jax.nn.relu(total)


def filter_costs(volume, conv_first, conv_second):
    tile_width = volume.shape[2]
    padded = with_halo(volume, (("tile", 2),), 1)
    first_out = conv_relu(padded, conv_first, tile_width)
    padded_first = with_halo(first_out, (("tile", 2),), 1)
    second_out = conv_relu(padded_first, conv_second, tile_width)
    return jnp.sum(second_out, axis=0)


def on_device(
    reference_feat, secondary_feat, pair_offsets, w_query_key, w_value, conv_first, conv_second
):
    tile_id = lax.axis_index("tile")
    cycle_size = lax.axis_size("tile")
    images = jnp.concatenate([reference_feat[None], secondary_feat], axis=0)
    features = neighborhood(images, w_query_key, w_value, tile_id, cycle_size)
    left_feat = features[0]
    right_window = secondary_window(features[1:])
    tile_width = left_feat.shape[1]
    score_sum = jnp.zeros((left_feat.shape[0], tile_width, DISP), jnp.float32)
    for pair_pos in range(secondary_feat.shape[0]):
        volume = correlate_local(
            left_feat, right_window[pair_pos], pair_offsets[pair_pos, 0], tile_width
        )
        score_sum = score_sum + filter_costs(volume, conv_first, conv_second)
    row_peak = jnp.max(score_sum, axis=-1, keepdims=True)
    disp_prob = jnp.exp(score_sum - row_peak)
    disp_prob = disp_prob / jnp.sum(disp_prob, axis=-1, keepdims=True)
    levels = jnp.arange(DISP, dtype=jnp.float32)
    return jnp.sum(disp_prob * levels, axis=-1) / DISP


def solution(mesh):
    return jax.shard_map(
        on_device,
        mesh=mesh,
        in_specs=(
            P("groups", "tile", None),
            P("groups", None, "tile", None),
            P("groups", "tile"),
            P(),
            P(),
            P(),
            P(),
        ),
        out_specs=P("groups", "tile"),
        check_vma=False,
    )
```

profile of v0, /device:TPU:1, one launch (start us, length us, event | category | flops | bytes accessed | tf_op | source)
XLA Modules:
  0.0 595.8 jit_solution(4516317373226120666)
XLA Ops:
  0.8 2.0 multiply_reduce_fusion
  4.9 4.5 collective-permute-start
  9.7 2.2 collective-permute-start.1
  34.9 2.1 fusion.31
  37.1 1.8 fusion.11
  39.0 1.9 collective-permute-start.2
  42.9 3.8 collective-permute-done.2
  46.8 1.8 collective-permute-start.3
  55.9 1.9 convolution_multiply_fusion
  57.8 2.4 reshape.2875
  61.9 4.3 reshape.2876
  67.2 3.3 collective-permute-start.8
  70.5 1.9 collective-permute-start.9
  72.4 1.8 convolution_multiply_fusion.1
  74.3 2.4 reshape.2872
  78.4 4.4 reshape.2873
  83.8 3.8 collective-permute-start.4
  87.5 2.1 collective-permute-start.5
  113.4 1.8 pad_slice_fusion.485
  119.1 1.8 pad_slice_fusion.449
  179.6 14.3 %multiply_add_fusion.1 = f32[8,4,64,128]{3,2,1,0:T(8,128)S(1)} fusion(f32[4,64,128]{2,1,0:T(8,128)S(1)} %get-tuple-element.765, f32[4,64,128]{2,1,0:T(8,128)S(1)} %pad.3039, f32[4,64,128]{2,1,0:T(8,128)S(1)} %pad.3038, f32[4,64,128]{2,1,0:T(8,128)S(1)} %get-tuple-element.764, f32[4,64,128]{2,1,0:T(8,128)S(1)} %pad.3037, f32[4,64,128]{2,1,0:T(8,128)S(1)} %pad.3036, ...), kind=kLoop, calls=%fused_computation.21 | loop fusion | flops 46399488 | bytes 12716832 | tf_op jit(solution)/shard_map/add | solution.py:132
  194.2 31.7 %add_maximum_fusion = f32[8,4,64,128]{3,2,1,0:T(8,128)S(1)} fusion(f32[8,4,64,128]{3,2,1,0:T(8,128)S(1)} %multiply_add_fusion.1, f32[4,64,128]{2,1,0:T(8,128)} %pad.3128, f32[4,64,128]{2,1,0:T(8,128)} %get-tuple-element.875, f32[4,64,128]{2,1,0:T(8,128)} %pad.3127, f32[4,64,128]{2,1,0:T(8,128)} %pad.3126, f32[4,64,128]{2,1,0:T(8,128)} %get-tuple-element.874, ...), kind=kLoop, calls=%fused_computation.20 | loop fusion | flops 66846720 | bytes 18747360 | tf_op jit(solution)/shard_map/jit(relu)/max | solution.py:133
  226.0 3.8 collective-permute-start.10
  229.8 2.1 collective-permute-start.11
  302.7 14.4 %multiply_add_fusion.3 = f32[8,4,64,128]{3,2,1,0:T(8,128)S(1)} fusion(f32[4,64,128]{2,1,0:T(8,128)S(1)} %copy-done.8, f32[8]{0:T(128)} %get-tuple-element.281, f32[4,64,128]{2,1,0:T(8,128)S(1)} %pad.2734, f32[8]{0:T(128)} %get-tuple-element.371, f32[4,64,128]{2,1,0:T(8,128)S(1)} %pad.2733, f32[8]{0:T(128)} %get-tuple-element.372, ...), kind=kLoop, calls=%fused_computation.25 | loop fusion | flops 46399488 | bytes 12716832 | tf_op jit(solution)/shard_map/add | solution.py:132
  317.2 25.2 %add_maximum_fusion.1 = f32[8,4,64,128]{3,2,1,0:T(8,128)S(1)} fusion(f32[8,4,64,128]{3,2,1,0:T(8,128)S(1)} %multiply_add_fusion.3, f32[4,64,128]{2,1,0:T(8,128)} %pad.2823, f32[8]{0:T(128)} %get-tuple-element.389, f32[4,64,128]{2,1,0:T(8,128)} %get-tuple-element.1307, f32[8]{0:T(128)} %get-tuple-element.370, f32[4,64,128]{2,1,0:T(8,128)} %pad.2822, ...), kind=kLoop, calls=%fused_computation.24 | loop fusion | flops 66846720 | bytes 18747360 | tf_op jit(solution)/shard_map/jit(relu)/max | solution.py:133
  342.4 3.9 collective-permute-start.6
  346.3 1.9 collective-permute-start.7
  507.8 15.3 %multiply_add_fusion = f32[8,4,64,128]{3,2,1,0:T(8,128)S(1)} fusion(f32[4,64,128]{2,1,0:T(8,128)S(1)} %pad.3192, f32[4,64,128]{2,1,0:T(8,128)S(1)} %get-tuple-element.549, f32[4,64,128]{2,1,0:T(8,128)S(1)} %pad.3191, f32[4,64,128]{2,1,0:T(8,128)S(1)} %pad.3190, f32[4,64,128]{2,1,0:T(8,128)S(1)} %get-tuple-element.548, f32[4,64,128]{2,1,0:T(8,128)S(1)} %pad.3189, ...), kind=kLoop, calls=%fused_computation.19 | loop fusion | flops 46923776 | bytes 12847936 | tf_op jit(solution)/shard_map/add | solution.py:132
  523.4 15.4 %multiply_add_fusion.2 = f32[8,4,64,128]{3,2,1,0:T(8,128)S(1)} fusion(f32[4,64,128]{2,1,0:T(8,128)} %pad.2887, f32[8]{0:T(128)} %get-tuple-element.64, f32[4,64,128]{2,1,0:T(8,128)} %get-tuple-element.981, f32[8]{0:T(128)} %get-tuple-element.65, f32[4,64,128]{2,1,0:T(8,128)} %pad.2886, f32[8]{0:T(128)} %get-tuple-element.155, f32[4,64,128]{2,1,0:T(8,128)} %pad.2885, ...), kind=kLoop, calls=%fused_computation.23 | loop fusion | flops 46923776 | bytes 12847936 | tf_op jit(solution)/shard_map/add | solution.py:132
  539.0 30.7 %maximum_reduce_fusion = f32[4,64,128]{2,1,0:T(8,128)} fusion(f32[8,4,64,128]{3,2,1,0:T(8,128)S(1)} %multiply_add_fusion, f32[4,64,128]{2,1,0:T(8,128)} %pad.3280, f32[4,64,128]{2,1,0:T(8,128)} %get-tuple-element.659, f32[4,64,128]{2,1,0:T(8,128)} %pad.3279, f32[4,64,128]{2,1,0:T(8,128)} %pad.3278, f32[4,64,128]{2,1,0:T(8,128)} %get-tuple-element.658, ...), kind=kLoop, calls=%fused_computation.18 | loop fusion | flops 66551808 | bytes 17698752 | tf_op jit(solution)/shard_map/reduce_sum | solution.py:142
  569.7 24.2 %maximum_reduce_fusion.1 = f32[4,64,128]{2,1,0:T(8,128)S(1)} fusion(f32[8,4,64,128]{3,2,1,0:T(8,128)S(1)} %multiply_add_fusion.2, f32[4,64,128]{2,1,0:T(8,128)} %pad.2975, f32[8]{0:T(128)S(1)} %get-tuple-element.173, f32[4,64,128]{2,1,0:T(8,128)} %get-tuple-element.1091, f32[8]{0:T(128)S(1)} %get-tuple-element.154, f32[4,64,128]{2,1,0:T(8,128)} %pad.2974, ...), kind=kLoop, calls=%fused_computation.22 | loop fusion | flops 66551808 | bytes 17698752 | tf_op jit(solution)/shard_map/reduce_sum | solution.py:142
  (1277 shorter events, 352.0 us)
Async XLA Ops:
  4.6 19.0 %copy-start.3 = (f32[8,8,3,3,3]{1,0,4,3,2:T(8,128)S(1)}, f32[8,8,3,3,3]{1,0,4,3,2:T(8,128)}, u32[]{:S(2)}) copy-start(f32[8,8,3,3,3]{1,0,4,3,2:T(8,128)} %param.13) | copy-start | bytes 20740
  4.9 28.1 %collective-permute-start = (f32[3,4,3,128]{3,1,2,0:T(4,128)S(1)}, f32[3,4,3,128]{3,1,2,0:T(4,128)S(1)}, u32[]{:S(2)}, u32[]{:S(2)}) collective-permute-start(f32[3,4,3,128]{3,1,2,0:T(4,128)S(1)} %copy.88), channel_id=1, source_target_pairs={{0,1},{1,2},{2,3},{3,4},{4,5},{5,6},{6,7},{7,8},{8,9},{9,10},{10,1... | collective-permute-start | bytes 55304 | tf_op jit(solution)/shard_map/ppermute | solution.py:23
  9.7 23.6 %collective-permute-start.1 = (f32[3,4,3,128]{3,1,2,0:T(4,128)S(1)}, f32[3,4,3,128]{3,1,2,0:T(4,128)S(1)}, u32[]{:S(2)}, u32[]{:S(2)}) collective-permute-start(f32[3,4,3,128]{3,1,2,0:T(4,128)S(1)} %copy.89), channel_id=1, source_target_pairs={{1,0},{2,1},{3,2},{4,3},{5,4},{6,5},{7,6},{8,7},{9,8},{10,9},{11,1... | collective-permute-start | bytes 55304 | tf_op jit(solution)/shard_map/ppermute | solution.py:24
  13.0 181.0 %copy-start.224 = (f32[8]{0:T(128)}, f32[8]{0:T(128)S(1)}, u32[]{:S(2)}) copy-start(f32[8]{0:T(128)S(1)} %get-tuple-element.263) | copy-start | bytes 100
  13.0 181.0 %copy-start.226 = (f32[8]{0:T(128)}, f32[8]{0:T(128)S(1)}, u32[]{:S(2)}) copy-start(f32[8]{0:T(128)S(1)} %get-tuple-element.264) | copy-start | bytes 100
  13.0 181.0 %copy-start.228 = (f32[8]{0:T(128)}, f32[8]{0:T(128)S(1)}, u32[]{:S(2)}) copy-start(f32[8]{0:T(128)S(1)} %get-tuple-element.265) | copy-start | bytes 100
  13.0 181.1 %copy-start.230 = (f32[8]{0:T(128)}, f32[8]{0:T(128)S(1)}, u32[]{:S(2)}) copy-start(f32[8]{0:T(128)S(1)} %get-tuple-element.266) | copy-start | bytes 100
  13.0 181.1 %copy-start.232 = (f32[8]{0:T(128)}, f32[8]{0:T(128)S(1)}, u32[]{:S(2)}) copy-start(f32[8]{0:T(128)S(1)} %get-tuple-element.267) | copy-start | bytes 100
  13.0 181.1 %copy-start.234 = (f32[8]{0:T(128)}, f32[8]{0:T(128)S(1)}, u32[]{:S(2)}) copy-start(f32[8]{0:T(128)S(1)} %get-tuple-element.268) | copy-start | bytes 100
  13.0 181.1 %copy-start.236 = (f32[8]{0:T(128)}, f32[8]{0:T(128)S(1)}, u32[]{:S(2)}) copy-start(f32[8]{0:T(128)S(1)} %get-tuple-element.269) | copy-start | bytes 100
  13.0 181.1 %copy-start.238 = (f32[8]{0:T(128)}, f32[8]{0:T(128)S(1)}, u32[]{:S(2)}) copy-start(f32[8]{0:T(128)S(1)} %get-tuple-element.270) | copy-start | bytes 100
  39.0 7.7 %collective-permute-start.2 = (f32[2,4,64,64]{2,3,1,0:T(8,128)S(1)}, f32[2,4,64,64]{2,3,1,0:T(8,128)S(1)}, u32[]{:S(2)}, u32[]{:S(2)}) collective-permute-start(f32[2,4,64,64]{2,3,1,0:T(8,128)S(1)} %slice.8241), channel_id=1, source_target_pairs={{1,0},{2,1},{3,2},{4,3},{5,4},{6,5},{7,6},{8,7},{9,8},{10,9},{11,1... | collective-permute-start | bytes 393224 | tf_op jit(solution)/shard_map/ppermute | solution.py:32
  46.8 8.6 %collective-permute-start.3 = (f32[2,4,128,64]{2,3,1,0:T(8,128)S(1)}, f32[2,4,128,64]{2,3,1,0:T(8,128)S(1)}, u32[]{:S(2)}, u32[]{:S(2)}) collective-permute-start(f32[2,4,128,64]{2,3,1,0:T(8,128)S(1)} %pad_maximum_fusion.10), channel_id=1, source_target_pairs={{2,0},{3,1},{4,2},{5,3},{6,4},{7,5},{8,6},{9,7},{10,8},{11,9},{12,... | collective-permute-start | bytes 786440 | tf_op jit(solution)/shard_map/ppermute | solution.py:32
  67.2 22.5 %collective-permute-start.8 = (f32[8,4,1,128]{3,2,1,0:T(1,128)S(1)}, f32[8,4,1,128]{3,2,1,0:T(1,128)S(1)}, u32[]{:S(2)}, u32[]{:S(2)}) collective-permute-start(f32[8,4,1,128]{3,2,1,0:T(1,128)S(1)} %get-tuple-element.482), channel_id=1, source_target_pairs={{0,1},{1,2},{2,3},{3,4},{4,5},{5,6},{6,7},{7,8},{8,9},{9,10},{10,1... | collective-permute-start | bytes 49160 | tf_op jit(solution)/shard_map/ppermute | solution.py:23
  70.5 19.2 %collective-permute-start.9 = (f32[8,4,1,128]{3,2,1,0:T(1,128)S(1)}, f32[8,4,1,128]{3,2,1,0:T(1,128)S(1)}, u32[]{:S(2)}, u32[]{:S(2)}) collective-permute-start(f32[8,4,1,128]{3,2,1,0:T(1,128)S(1)} %get-tuple-element.483), channel_id=1, source_target_pairs={{1,0},{2,1},{3,2},{4,3},{5,4},{6,5},{7,6},{8,7},{9,8},{10,9},{11,1... | collective-permute-start | bytes 49160 | tf_op jit(solution)/shard_map/ppermute | solution.py:24
  83.8 14.9 %collective-permute-start.4 = (f32[8,4,1,128]{3,2,1,0:T(1,128)S(1)}, f32[8,4,1,128]{3,2,1,0:T(1,128)S(1)}, u32[]{:S(2)}, u32[]{:S(2)}) collective-permute-start(f32[8,4,1,128]{3,2,1,0:T(1,128)S(1)} %get-tuple-element.484), channel_id=1, source_target_pairs={{0,1},{1,2},{2,3},{3,4},{4,5},{5,6},{6,7},{7,8},{8,9},{9,10},{10,1... | collective-permute-start | bytes 49160 | tf_op jit(solution)/shard_map/ppermute | solution.py:23
  87.5 11.1 %collective-permute-start.5 = (f32[8,4,1,128]{3,2,1,0:T(1,128)S(1)}, f32[8,4,1,128]{3,2,1,0:T(1,128)S(1)}, u32[]{:S(2)}, u32[]{:S(2)}) collective-permute-start(f32[8,4,1,128]{3,2,1,0:T(1,128)S(1)} %get-tuple-element.485), channel_id=1, source_target_pairs={{1,0},{2,1},{3,2},{4,3},{5,4},{6,5},{7,6},{8,7},{9,8},{10,9},{11,1... | collective-permute-start | bytes 49160 | tf_op jit(solution)/shard_map/ppermute | solution.py:24
  226.0 122.2 %collective-permute-start.10 = (f32[8,4,1,128]{3,2,1,0:T(1,128)S(1)}, f32[8,4,1,128]{3,2,1,0:T(1,128)S(1)}, u32[]{:S(2)}, u32[]{:S(2)}) collective-permute-start(f32[8,4,1,128]{3,2,1,0:T(1,128)S(1)} %get-tuple-element.518), channel_id=1, source_target_pairs={{0,1},{1,2},{2,3},{3,4},{4,5},{5,6},{6,7},{7,8},{8,9},{9,10},{10,1... | collective-permute-start | bytes 49160 | tf_op jit(solution)/shard_map/ppermute | solution.py:23
  229.8 118.5 %collective-permute-start.11 = (f32[8,4,1,128]{3,2,1,0:T(1,128)S(1)}, f32[8,4,1,128]{3,2,1,0:T(1,128)S(1)}, u32[]{:S(2)}, u32[]{:S(2)}) collective-permute-start(f32[8,4,1,128]{3,2,1,0:T(1,128)S(1)} %get-tuple-element.519), channel_id=1, source_target_pairs={{1,0},{2,1},{3,2},{4,3},{5,4},{6,5},{7,6},{8,7},{9,8},{10,9},{11,1... | collective-permute-start | bytes 49160 | tf_op jit(solution)/shard_map/ppermute | solution.py:24
  342.4 17.6 %collective-permute-start.6 = (f32[8,4,1,128]{3,2,1,0:T(1,128)S(1)}, f32[8,4,1,128]{3,2,1,0:T(1,128)S(1)}, u32[]{:S(2)}, u32[]{:S(2)}) collective-permute-start(f32[8,4,1,128]{3,2,1,0:T(1,128)S(1)} %get-tuple-element.520), channel_id=1, source_target_pairs={{0,1},{1,2},{2,3},{3,4},{4,5},{5,6},{6,7},{7,8},{8,9},{9,10},{10,1... | collective-permute-start | bytes 49160 | tf_op jit(solution)/shard_map/ppermute | solution.py:23
  346.3 13.6 %collective-permute-start.7 = (f32[8,4,1,128]{3,2,1,0:T(1,128)S(1)}, f32[8,4,1,128]{3,2,1,0:T(1,128)S(1)}, u32[]{:S(2)}, u32[]{:S(2)}) collective-permute-start(f32[8,4,1,128]{3,2,1,0:T(1,128)S(1)} %get-tuple-element.521), channel_id=1, source_target_pairs={{1,0},{2,1},{3,2},{4,3},{5,4},{6,5},{7,6},{8,7},{9,8},{10,9},{11,1... | collective-permute-start | bytes 49160 | tf_op jit(solution)/shard_map/ppermute | solution.py:24
  523.1 15.6 %copy-start.176 = (f32[8]{0:T(128)S(1)}, f32[8]{0:T(128)}, u32[]{:S(2)}) copy-start(f32[8]{0:T(128)} %get-tuple-element.57) | copy-start | bytes 100
  523.1 15.6 %copy-start.177 = (f32[8]{0:T(128)S(1)}, f32[8]{0:T(128)}, u32[]{:S(2)}) copy-start(f32[8]{0:T(128)} %get-tuple-element.58) | copy-start | bytes 100
  523.1 15.6 %copy-start.178 = (f32[8]{0:T(128)S(1)}, f32[8]{0:T(128)}, u32[]{:S(2)}) copy-start(f32[8]{0:T(128)} %get-tuple-element.59) | copy-start | bytes 100
  523.1 15.6 %copy-start.179 = (f32[8]{0:T(128)S(1)}, f32[8]{0:T(128)}, u32[]{:S(2)}) copy-start(f32[8]{0:T(128)} %get-tuple-element.60) | copy-start | bytes 100
  523.2 15.6 %copy-start.180 = (f32[8]{0:T(128)S(1)}, f32[8]{0:T(128)}, u32[]{:S(2)}) copy-start(f32[8]{0:T(128)} %get-tuple-element.61) | copy-start | bytes 100
  523.2 15.6 %copy-start.181 = (f32[8]{0:T(128)S(1)}, f32[8]{0:T(128)}, u32[]{:S(2)}) copy-start(f32[8]{0:T(128)} %get-tuple-element.62) | copy-start | bytes 100
  523.2 15.6 %copy-start.182 = (f32[8]{0:T(128)S(1)}, f32[8]{0:T(128)}, u32[]{:S(2)}) copy-start(f32[8]{0:T(128)} %get-tuple-element.63) | copy-start | bytes 100
  523.2 15.6 %copy-start.183 = (f32[8]{0:T(128)S(1)}, f32[8]{0:T(128)}, u32[]{:S(2)}) copy-start(f32[8]{0:T(128)} %get-tuple-element.85) | copy-start | bytes 100
  523.2 15.6 %copy-start.184 = (f32[8]{0:T(128)S(1)}, f32[8]{0:T(128)}, u32[]{:S(2)}) copy-start(f32[8]{0:T(128)} %get-tuple-element.86) | copy-start | bytes 100
  523.2 15.6 %copy-start.185 = (f32[8]{0:T(128)S(1)}, f32[8]{0:T(128)}, u32[]{:S(2)}) copy-start(f32[8]{0:T(128)} %get-tuple-element.87) | copy-start | bytes 100
  569.7 25.9 %copy-start.1 = (f32[256,64]{0,1:T(8,128)S(1)}, f32[256,64]{0,1:T(8,128)}, u32[]{:S(2)}) copy-start(f32[256,64]{0,1:T(8,128)} %param.10) | copy-start | bytes 196612
  (263 other events, 1784.4 us)
where the time goes:
time: 603 us; the launch traced here: 596 us
  local copies, waits for them, and re-layouts  363 us (60%)
  other arithmetic  180 us (30%)
  starting transfers between devices  33.3 us (6%)
  between operations  8.86 us (1%)
  matrix products  6.91 us (1%)
    pad x288, local copies, waits for them, and re-layouts, tap_view(): return jnp.pad(rowed[:, :, :-1], ((0, 0), (0, 0), (1, 0)))  140 us
    pad x288, local copies, waits for them, and re-layouts, tap_view(): return jnp.pad(rowed[:, :, 1:], ((0, 0), (0, 0), (0, 1)))  118 us
    add x4, other arithmetic, conv_relu(): total = term if total is None else total + term  59.4 us
    max x2, other arithmetic, conv_relu(): return jax.nn.relu(total)  56.9 us
    reduce_sum x2, other arithmetic, filter_costs(): return jnp.sum(second_out, axis=0)  54.9 us
    slice x32, local copies, waits for them, and re-layouts, tap_view(): jnp.pad(plane, ((1, 1), (0, 0), (0, 0)))  31.1 us
    slice x24, local copies, waits for them, and re-layouts, conv_relu(): weights[:, in_pos, row_tap, col_tap, disp_tap][:, None, None, None]  24.9 us
    slice x30, local copies, waits for them, and re-layouts, tap_view(): return jnp.pad(rowed[:, :, :-1], ((0, 0), (0, 0), (1, 0)))  21.2 us
  transfers between devices with their start and end apart: 12, of which 2 were waited for; matrix products, arithmetic and copies ran while one was open for 28% of the time, Pallas kernels for 0%

commit v1 on v0

v1 whole, which is shorter than its diff:
```python
import functools

import jax
import jax.numpy as jnp
from jax import lax
from jax.experimental import pallas as pl
from jax.experimental.pallas import tpu as pltpu
from jax.sharding import PartitionSpec as P

GROUPS = 8
DISP = 128
RAD = 3
ROWS = 4
CH = 64
LANES = ROWS * CH
HALO = 8
F32 = jnp.float32
BF16 = jnp.bfloat16


def dot(a, b):
    return jnp.dot(a, b, preferred_element_type=F32)


def split2(x):
    hi = x.astype(BF16)
    return hi, (x - hi.astype(F32)).astype(BF16)


def split3(x):
    hi = x.astype(BF16)
    rest = x - hi.astype(F32)
    mid = rest.astype(BF16)
    return hi, mid, (rest - mid.astype(F32)).astype(BF16)


def attend_kernel(images, width, info, ref, sec, left, right, wq, wv, out_ref, out_sec, out_halo, stacked, weights, query, value, scores):
    wide = width + 2 * HALO
    first_col, total_cols = info[0], info[1]
    weights[:, :CH] = wq[...]
    weights[:, CH:] = wv[...]
    zeros = jnp.zeros((HALO, LANES), F32)
    for image in range(images):
        for row in range(ROWS):
            base = row * wide
            stacked[base:base + HALO, :] = left[image, row]
            stacked[base + HALO:base + HALO + width, :] = ref[row] if image == 0 else sec[image - 1, row]
            stacked[base + HALO + width:base + wide, :] = right[image, row]
        both = jnp.dot(stacked[...], weights[...], precision=lax.Precision.HIGHEST, preferred_element_type=F32)
        for row in range(ROWS):
            part = both[row * wide:(row + 1) * wide, :]
            query[HALO:HALO + wide, row * CH:(row + 1) * CH] = part[:, :CH]
            value[HALO:HALO + wide, row * CH:(row + 1) * CH] = part[:, CH:]
        for buffer in (query, value):
            buffer[0:HALO, :] = zeros
            buffer[HALO + wide:, :] = zeros
        lane_row = lax.broadcasted_iota(jnp.int32, (wide, LANES), 1) // CH
        column = lax.broadcasted_iota(jnp.int32, (wide, LANES), 0) + (first_col - HALO)
        ones = jnp.where(
            lax.broadcasted_iota(jnp.int32, (LANES, LANES), 0) // CH
            == lax.broadcasted_iota(jnp.int32, (LANES, LANES), 1) // CH,
            1.0 / CH, 0.0).astype(BF16)
        own = query[HALO:HALO + wide, :]
        peak = jnp.full((wide, LANES), -1e30, F32)
        place = 0
        for shift in range(-RAD, RAD + 1):
            keys = query[HALO + shift:HALO + shift + wide, :]
            col_ok = (column + shift >= 0) & (column + shift < total_cols)
            for step in (-1, 0, 1):
                moved = pltpu.roll(keys, (-step * CH) % LANES, 1) if step else keys
                hi, mid, low = split3(own * moved)
                score = dot(hi, ones) + dot(mid, ones) + dot(low, ones)
                row_ok = (lane_row + step >= 0) & (lane_row + step < ROWS)
                score = jnp.where(col_ok & row_ok, score, -1e30)
                scores[place] = score
                peak = jnp.maximum(peak, score)
                place += 1
        total = jnp.zeros((wide, LANES), F32)
        mixed = jnp.zeros((wide, LANES), F32)
        place = 0
        for shift in range(-RAD, RAD + 1):
            vals = value[HALO + shift:HALO + shift + wide, :]
            for step in (-1, 0, 1):
                moved = pltpu.roll(vals, (-step * CH) % LANES, 1) if step else vals
                weight = jnp.exp(scores[place] - peak)
                total = total + weight
                mixed = mixed + weight * moved
                place += 1
        feature = value[HALO:HALO + wide, :] + mixed / total
        if image == 0:
            out_ref[...] = jnp.where((column >= 0) & (column < total_cols), feature, 0.0)
        else:
            out_halo[image - 1] = feature[:HALO]
            out_sec[image - 1] = feature[HALO:HALO + width]


def cost_kernel(pairs, width, info, taps, feat, halo, sec0, sec1, sec2, sec3, out,
                window, moved, padded, prod, plane, high, low, w_high, w_low):
    group = ROWS * GROUPS
    blocks = width // 8
    block = 8 * group
    span = 10 * group
    full = (width + 4) * group
    tail = blocks * block
    tiles = DISP + 16
    window[...] = jnp.zeros_like(window)
    for pair in range(pairs):
        window[pair, 0:HALO, :] = halo[pair]
        for place, sec in enumerate((sec0, sec1, sec2, sec3)):
            window[pair, HALO + place * width:HALO + (place + 1) * width, :] = sec[pair]
        plane[pair, 0:8, :] = jnp.zeros((8, full), F32)
        plane[pair, 8 + DISP:, :] = jnp.zeros((8, full), F32)
    padded[...] = jnp.zeros_like(padded)
    padded[0:width + 2 * HALO, :] = feat[...]
    for conv in range(2):
        for tap in range(3):
            w_high[conv, tap] = jnp.zeros((span, block), BF16)
            w_low[conv, tap] = jnp.zeros((span, block), BF16)
            hi, lo = split2(taps[conv, tap])
            for col in range(8):
                at = (slice(col * group, (col + 3) * group), slice(col * group, (col + 1) * group))
                w_high[(conv, tap) + at] = hi
                w_low[(conv, tap) + at] = lo
    feat_hi, feat_lo = split2(padded[...].T)
    lane = lax.broadcasted_iota(jnp.int32, (DISP, 128), 1)

    def left_matrix(at):
        rows = lax.broadcasted_iota(jnp.int32, (128, block), 0)
        lanes = lax.broadcasted_iota(jnp.int32, (128, block), 1)
        spread = jnp.where(rows == lanes // group + (8 * at + HALO - 2), 1.0, 0.0).astype(BF16)
        keep = jnp.where(
            lax.broadcasted_iota(jnp.int32, (LANES, block), 0) // GROUPS
            == lax.broadcasted_iota(jnp.int32, (LANES, block), 1) % group,
            1.0 / (CH // GROUPS), 0.0)
        return (dot(feat_hi, spread) * keep).astype(BF16), (dot(feat_lo, spread) * keep).astype(BF16)

    def shifted(pair, offset, start, count):
        first = offset + (HALO - 2)
        rest = first % 8
        aligned = pl.multiple_of(first - rest + start, 8)
        rows = window[pair, pl.ds(aligned, count + 8), :]
        return pltpu.roll(rows, count + 8 - rest, 0)[:count]

    def skewed(rows, left_hi, left_lo, halves):
        right_hi, right_lo = split2(rows)
        prod[...] = dot(right_hi, left_hi) + dot(right_hi, left_lo) + dot(right_lo, left_hi)
        result = []
        for half in range(halves):
            lanes = slice(half * 128, (half + 1) * 128)
            value = prod[half * 4:half * 4 + DISP, lanes]
            for col in range(1, 4):
                other = prod[half * 4 + col:half * 4 + col + DISP, lanes]
                value = jnp.where(lane >= col * group, other, value)
            result.append(value)
        return result

    for pair in range(pairs):
        moved[pair] = shifted(pair, info[3 * pair], 0, width + tiles)

    def volume_step(at, carry):
        left_hi, left_lo = left_matrix(at)
        for pair in range(pairs):
            parts = skewed(moved[pair, pl.ds(pl.multiple_of(8 * at, 8), tiles), :], left_hi, left_lo, 2)
            for half in range(2):
                plane[pair, 8:8 + DISP, pl.ds(pl.multiple_of(at * block + half * 128, 128), 128)] = parts[half]
        return carry

    lax.fori_loop(0, blocks, volume_step, 0)
    left_hi, left_lo = left_matrix(0)
    for pair in range(pairs):
        (edge,) = skewed(shifted(pair, info[3 * pair + 1], 0, tiles), left_hi, left_lo, 1)
        plane[pair, 8:8 + DISP, 0:128] = jnp.where(lane < 2 * group, edge, plane[pair, 8:8 + DISP, 0:128])
    left_hi, left_lo = left_matrix(blocks)
    for pair in range(pairs):
        (mine,) = skewed(moved[pair, width:width + tiles, :], left_hi, left_lo, 1)
        (edge,) = skewed(shifted(pair, info[3 * pair + 2], width, tiles), left_hi, left_lo, 1)
        plane[pair, 8:8 + DISP, tail:tail + 128] = jnp.where(lane < 2 * group, mine, edge)

    def split_planes():
        def step(at, carry):
            lanes = pl.ds(pl.multiple_of(at * 128, 128), 128)
            for pair in range(pairs):
                for tap in range(3):
                    hi, lo = split2(plane[pair, 7 + tap:7 + tap + DISP, lanes])
                    high[tap, pair * DISP:(pair + 1) * DISP, lanes] = hi
                    low[tap, pair * DISP:(pair + 1) * DISP, lanes] = lo
            return carry

        lax.fori_loop(0, full // 128, step, 0)

    def conv(which, start, depth, count):
        total = None
        lanes = pl.ds(start, depth)
        for tap in range(3):
            hi = high[tap, :, lanes]
            lo = low[tap, :, lanes]
            wh = w_high[which, tap, 0:depth, 0:count]
            wl = w_low[which, tap, 0:depth, 0:count]
            term = dot(hi, wh) + dot(hi, wl) + dot(lo, wh)
            total = term if total is None else total + term
        return jnp.maximum(total, 0.0)

    split_planes()
    is_first, is_last = info[3 * pairs], info[3 * pairs + 1]

    def first_step(at, carry):
        start = pl.multiple_of(at * block, block)
        result = conv(0, start, span, block)
        lanes = lax.broadcasted_iota(jnp.int32, result.shape, 1)
        result = jnp.where((lanes < group) & (is_first + jnp.where(at == 0, 1, 0) == 2), 0.0, result)
        for pair in range(pairs):
            plane[pair, 8:8 + DISP, pl.ds(start, block)] = result[pair * DISP:(pair + 1) * DISP]
        return carry

    lax.fori_loop(0, blocks, first_step, 0)
    result = conv(0, tail, 128, 128)
    lanes = lax.broadcasted_iota(jnp.int32, result.shape, 1)
    result = jnp.where((lanes >= group) & (is_last == 1), 0.0, result)
    for pair in range(pairs):
        plane[pair, 8:8 + DISP, tail:tail + 128] = result[pair * DISP:(pair + 1) * DISP]
    split_planes()
    level = lax.broadcasted_iota(jnp.int32, (DISP, block), 0).astype(F32)

    def second_step(at, carry):
        result = conv(1, pl.multiple_of(at * block, block), span, block)
        score = result[:DISP]
        for pair in range(1, pairs):
            score = score + result[pair * DISP:(pair + 1) * DISP]
        for shift in (4, 2, 1):
            score = score + pltpu.roll(score, block - shift, 1)
        weight = jnp.exp(score - jnp.max(score, axis=0, keepdims=True))
        mean = jnp.sum(weight * level, axis=0, keepdims=True) / jnp.sum(weight, axis=0, keepdims=True)
        out[pl.ds(at, 1), :] = mean / DISP
        return carry

    lax.fori_loop(0, blocks, second_step, 0)


def passed_along(value, axis, steps):
    count = lax.axis_size(axis)
    first, last = (max(0, -steps), min(count, count - steps))
    return lax.ppermute(value, axis, [(source, source + steps) for source in range(first, last)])


def tap_matrices(conv_first, conv_second):
    both = jnp.stack([conv_first, conv_second])
    flipped = jnp.transpose(both, (0, 5, 4, 3, 2, 1))
    rows = jnp.pad(flipped, ((0, 0), (0, 0), (0, 0), (ROWS - 1, ROWS - 1), (0, 0), (0, 0)))
    parts = [rows[:, :, :, ROWS - out:2 * ROWS - out] for out in range(ROWS)]
    joined = jnp.concatenate(parts, axis=-1)
    return joined.reshape(2, 3, 3 * ROWS * GROUPS, ROWS * GROUPS)


def on_device(reference_feat, secondary_feat, pair_offsets, w_query_key, w_value, conv_first, conv_second):
    pairs = secondary_feat.shape[0]
    images = pairs + 1
    width = reference_feat.shape[1]
    tile_id = lax.axis_index("tile")
    count = lax.axis_size("tile")
    wide = width + 2 * HALO
    group = ROWS * GROUPS
    full = (width + 4) * group
    vmem = pl.BlockSpec(memory_space=pltpu.VMEM)
    smem = pl.BlockSpec(memory_space=pltpu.SMEM)
    ends = jnp.concatenate([reference_feat[None, :, -HALO:], secondary_feat[:, :, -HALO:]], axis=0)
    starts = jnp.concatenate([reference_feat[None, :, :HALO], secondary_feat[:, :, :HALO]], axis=0)
    left = passed_along(ends, "tile", 1)
    right = passed_along(starts, "tile", -1)
    before = passed_along(pair_offsets, "tile", 1)
    after = passed_along(pair_offsets, "tile", -1)
    taps = tap_matrices(conv_first, conv_second)
    place = jnp.stack([tile_id * width, count * width]).astype(jnp.int32)
    feat, own, halo = pl.pallas_call(
        functools.partial(attend_kernel, images, width),
        out_shape=(
            jax.ShapeDtypeStruct((wide, LANES), F32),
            jax.ShapeDtypeStruct((pairs, width, LANES), F32),
            jax.ShapeDtypeStruct((pairs, HALO, LANES), F32),
        ),
        in_specs=[smem] + [vmem] * 6,
        out_specs=(vmem, vmem, vmem),
        scratch_shapes=[
            pltpu.VMEM((ROWS * wide, reference_feat.shape[2]), F32),
            pltpu.VMEM((reference_feat.shape[2], 2 * CH), F32),
            pltpu.VMEM((wide + 2 * HALO, LANES), F32),
            pltpu.VMEM((wide + 2 * HALO, LANES), F32),
            pltpu.VMEM((3 * (2 * RAD + 1), wide, LANES), F32),
        ],
        compiler_params=pltpu.CompilerParams(vmem_limit_bytes=24 << 20),
    )(place, reference_feat, secondary_feat, left, right, w_query_key, w_value)
    nexts = [passed_along(own, "tile", -step) for step in (1, 2, 3)]
    info = jnp.concatenate([
        jnp.concatenate([pair_offsets, before, after], axis=1).reshape(-1),
        jnp.stack([tile_id == 0, tile_id == count - 1]).astype(jnp.int32),
    ])
    result = pl.pallas_call(
        functools.partial(cost_kernel, pairs, width),
        out_shape=jax.ShapeDtypeStruct((width // 8, 8 * group), F32),
        in_specs=[smem] + [vmem] * 7,
        out_specs=vmem,
        scratch_shapes=[
            pltpu.VMEM((pairs, HALO + 4 * width + 16, LANES), F32),
            pltpu.VMEM((pairs, width + DISP + 16, LANES), F32),
            pltpu.VMEM((128, LANES), F32),
            pltpu.VMEM((DISP + 16, 8 * group), F32),
            pltpu.VMEM((pairs, DISP + 16, full), F32),
            pltpu.VMEM((3, pairs * DISP, full), BF16),
            pltpu.VMEM((3, pairs * DISP, full), BF16),
            pltpu.VMEM((2, 3, 10 * group, 8 * group), BF16),
            pltpu.VMEM((2, 3, 10 * group, 8 * group), BF16),
        ],
        compiler_params=pltpu.CompilerParams(vmem_limit_bytes=48 << 20),
    )(info, taps, feat, halo, own, *nexts)
    values = result.reshape(width // 8, 8, ROWS, GROUPS)[..., 0]
    return jnp.transpose(values, (2, 0, 1)).reshape(ROWS, width)


def solution(mesh):
    return jax.shard_map(
        on_device,
        mesh=mesh,
        in_specs=(
            P("groups", "tile", None),
            P("groups", None, "tile", None),
            P("groups", "tile"),
            P(),
            P(),
            P(),
            P(),
        ),
        out_specs=P("groups", "tile"),
        check_vma=False,
    )
```

time: 603 us -> 68.2 us (0.11); the launches traced: 596 us -> 67.7 us
  local copies, waits for them, and re-layouts: 363 us -> 4.93 us
  other arithmetic: 180 us -> 0.57 us
  Pallas kernels: 0 us -> 34.6 us
  starting transfers between devices: 33.3 us -> 16.8 us
  between operations: 8.86 us -> 0.25 us
  matrix products: 6.91 us -> 0 us
  waiting for transfers between devices: 4.22 us -> 10.6 us
    pad x578 -> x0, local copies, waits for them, and re-layouts: 261 us -> none  [the longest x288 140 us: tap_view(): return jnp.pad(rowed[:, :, :-1], ((0, 0), (0, 0), (1, 0)))]
    slice x103 -> x2, local copies, waits for them, and re-layouts: 83.1 us -> 0.98 us  [the longest x1 0.88 us: on_device(): secondary_feat[:, :, :HALO]]
    add x6 -> x0, other arithmetic: 61.3 us -> none  [the longest x4 59.4 us: conv_relu(): total = term if total is None else total + term]
    reduce_sum x4 -> x0, other arithmetic: 57.3 us -> none  [the longest x2 54.9 us: filter_costs(): return jnp.sum(second_out, axis=0)]
    max x2 -> x0, other arithmetic: 56.9 us -> none  [conv_relu(): return jax.nn.relu(total)]
    pallas_call x0 -> x2, Pallas kernels: none -> 34.6 us  [the longest x1 27.2 us: on_device(): pl.pallas_call(functools.partial(cost_kernel, pairs, width), out_shape=ja...]
    ppermute x10 -> x0, starting transfers between devices: 29.6 us -> none  [the longest x5 19.4 us: with_halo(): before = lax.ppermute(last, axis, up)]
    ppermute x2 -> x7, starting transfers between devices: 3.74 us -> 16.8 us  [passed_along(): lax.ppermute(value, axis, [(source, source + steps) for source in range(f...]
  transfers between devices with their start and end apart: 12 -> 7, of which waited for: 2 -> 4; matrix products, arithmetic and copies ran while one was open for 28% -> 3% of each run, Pallas kernels for 0% -> 11%
where the time goes in v1:
time: 68.2 us; the launch traced here: 67.7 us
  Pallas kernels  34.6 us (51%)
  starting transfers between devices  16.8 us (25%)
  waiting for transfers between devices  10.6 us (16%)
  local copies, waits for them, and re-layouts  4.93 us (7%)
    pallas_call x1, Pallas kernels, on_device(): pl.pallas_call(functools.partial(cost_kernel, pairs, width), out_shape=ja...  27.2 us
    ppermute x7, starting transfers between devices, passed_along(): lax.ppermute(value, axis, [(source, source + steps) for source in range(f...  16.8 us
    ppermute x7, waiting for transfers between devices, passed_along(): lax.ppermute(value, axis, [(source, source + steps) for source in range(f...  10.6 us
    pallas_call x1, Pallas kernels, on_device(): pl.pallas_call(functools.partial(attend_kernel, images, width), out_shape...  7.41 us
    unnamed x19, local copies, waits for them, and re-layouts  2.89 us
  transfers between devices with their start and end apart: 7, of which 4 were waited for; matrix products, arithmetic and copies ran while one was open for 3% of the time, Pallas kernels for 11%

profile of v1, /device:TPU:1, one launch (start us, length us, event | category | flops | bytes accessed | tf_op | source)
XLA Modules:
  0.0 67.7 jit_solution(1450493670177572650)
XLA Ops:
  0.0 4.7 %collective-permute-start = (s32[2,1]{0,1:T(1,128)}, s32[2,1]{0,1:T(1,128)S(1)}, u32[]{:S(2)}, u32[]{:S(2)}) collective-permute-start(s32[2,1]{0,1:T(1,128)} %param.9), channel_id=1, source_target_pairs={{0,1},{1,2},{2,3},{3,4},{4,5},{5,6},{6,7},{7,8},{8,9},{9,10},{10,1... | collective-permute-start | bytes 32 | tf_op jit(solution)/shard_map/ppermute | solution.py:242
  4.7 1.9 %collective-permute-start.1 = (s32[2,1]{0,1:T(1,128)}, s32[2,1]{0,1:T(1,128)S(1)}, u32[]{:S(2)}, u32[]{:S(2)}) collective-permute-start(s32[2,1]{0,1:T(1,128)} %param.9), channel_id=1, source_target_pairs={{1,0},{2,1},{3,2},{4,3},{5,4},{6,5},{7,6},{8,7},{9,8},{10,9},{11,1... | collective-permute-start | bytes 32 | tf_op jit(solution)/shard_map/ppermute | solution.py:242
  6.6 0.9 %fusion = (f32[2,4,8,256]{3,2,1,0:T(8,128)S(1)}, f32[2,4,8,256]{3,2,1,0:T(8,128)S(1)}) fusion(f32[2,4,64,256]{3,2,1,0:T(8,128)} %sec.1), kind=kLoop, calls=%fused_computation.14 | loop fusion | bytes 262144 | tf_op jit(solution)/shard_map/slice | solution.py:266
  7.5 3.8 %collective-permute-start.2 = (f32[3,4,8,256]{3,2,1,0:T(8,128)S(1)}, f32[3,4,8,256]{3,2,1,0:T(8,128)S(1)}, u32[]{:S(2)}, u32[]{:S(2)}) collective-permute-start(f32[3,4,8,256]{3,2,1,0:T(8,128)S(1)} %pad_maximum_fusion.1), channel_id=1, source_target_pairs={{0,1},{1,2},{2,3},{3,4},{4,5},{5,6},{6,7},{7,8},{8,9},{9,10},{10,1... | collective-permute-start | bytes 294920 | tf_op jit(solution)/shard_map/ppermute | solution.py:242
  11.3 1.9 %collective-permute-start.3 = (f32[3,4,8,256]{3,2,1,0:T(8,128)S(1)}, f32[3,4,8,256]{3,2,1,0:T(8,128)S(1)}, u32[]{:S(2)}, u32[]{:S(2)}) collective-permute-start(f32[3,4,8,256]{3,2,1,0:T(8,128)S(1)} %pad_maximum_fusion.2), channel_id=1, source_target_pairs={{1,0},{2,1},{3,2},{4,3},{5,4},{6,5},{7,6},{8,7},{9,8},{10,9},{11,1... | collective-permute-start | bytes 294920 | tf_op jit(solution)/shard_map/ppermute | solution.py:242
  13.3 0.0 copy-start.3
  13.3 0.1 copy.19
  13.4 0.8 %copy-done.3 = f32[8,8,3,3,3]{1,0,4,3,2:T(8,128)S(1)} copy-done((f32[8,8,3,3,3]{1,0,4,3,2:T(8,128)S(1)}, f32[8,8,3,3,3]{1,0,4,3,2:T(8,128)}, u32[]{:S(2)}) %copy-start.3) | copy-done | bytes 6936
  14.2 0.1 copy.20
  14.3 0.1 pad_slice_fusion.3
  14.4 0.7 %copy-done.4 = f32[256,64]{0,1:T(8,128)S(1)} copy-done((f32[256,64]{0,1:T(8,128)S(1)}, f32[256,64]{0,1:T(8,128)}, u32[]{:S(2)}) %copy-start.4) | copy-done | bytes 65560
  15.1 0.1 copy.21.wq
  15.2 0.7 %copy-done.5 = f32[256,64]{0,1:T(8,128)S(1)} copy-done((f32[256,64]{0,1:T(8,128)S(1)}, f32[256,64]{0,1:T(8,128)}, u32[]{:S(2)}) %copy-start.5) | copy-done | bytes 65560
  16.0 0.1 copy.22.wv
  16.1 0.1 pad_add_fusion.2.info
  16.2 0.3 pad_maximum_fusion
  16.5 0.1 add_convert_fusion
  16.5 0.7 %collective-permute-done.3.right = f32[3,4,8,256]{3,2,1,0:T(8,128)S(1)} collective-permute-done((f32[3,4,8,256]{3,2,1,0:T(8,128)S(1)}, f32[3,4,8,256]{3,2,1,0:T(8,128)S(1)}, u32[]{:S(2)}, u32[]{:S(2)}) %collective-permute-start.3) | collective-permute-done | bytes 98336 | tf_op jit(solution)/shard_map/ppermute | solution.py:242
  17.3 7.4 %shard_map.73 = (f32[80,256]{1,0:T(8,128)S(1)}, f32[2,64,256]{2,1,0:T(8,128)S(1)}, f32[2,8,256]{2,1,0:T(8,128)S(1)}) custom-call(s32[2]{0:T(128)S(1)} %pad_add_fusion.2.info, f32[4,64,256]{2,1,0:T(8,128)S(1)} %copy-done.1, f32[2,4,64,256]{3,2,1,0:T(8,128)S(1)} %copy-done, f32[3,4,8,256]{3,2,1,0:T(8,128)S(1)} %collective-permute-done.2.left, ...), custom_call_target="tpu_custom_call" | custom-call | tf_op jit(solution)/shard_map/pallas_call | solution.py:273
  24.7 1.9 %collective-permute-start.4 = (f32[2,64,256]{2,1,0:T(8,128)S(1)}, f32[2,64,256]{2,1,0:T(8,128)S(1)}, u32[]{:S(2)}, u32[]{:S(2)}) collective-permute-start(f32[2,64,256]{2,1,0:T(8,128)S(1)} %get-tuple-element.10.sec0), channel_id=1, source_target_pairs={{1,0},{2,1},{3,2},{4,3},{5,4},{6,5},{7,6},{8,7},{9,8},{10,9},{11,1... | collective-permute-start | bytes 393224 | tf_op jit(solution)/shard_map/ppermute | solution.py:242
  26.6 1.3 %collective-permute-start.5 = (f32[2,64,256]{2,1,0:T(8,128)S(1)}, f32[2,64,256]{2,1,0:T(8,128)S(1)}, u32[]{:S(2)}, u32[]{:S(2)}) collective-permute-start(f32[2,64,256]{2,1,0:T(8,128)S(1)} %get-tuple-element.10.sec0), channel_id=1, source_target_pairs={{2,0},{3,1},{4,2},{5,3},{6,4},{7,5},{8,6},{9,7},{10,8},{11,9},{12,... | collective-permute-start | bytes 393224 | tf_op jit(solution)/shard_map/ppermute | solution.py:242
  27.9 1.3 %collective-permute-start.6 = (f32[2,64,256]{2,1,0:T(8,128)S(1)}, f32[2,64,256]{2,1,0:T(8,128)S(1)}, u32[]{:S(2)}, u32[]{:S(2)}) collective-permute-start(f32[2,64,256]{2,1,0:T(8,128)S(1)} %get-tuple-element.10.sec0), channel_id=1, source_target_pairs={{3,0},{4,1},{5,2},{6,3},{7,4},{8,5},{9,6},{10,7},{11,8},{12,9},{13... | collective-permute-start | bytes 393224 | tf_op jit(solution)/shard_map/ppermute | solution.py:242
  29.3 0.1 copy.18
  29.4 0.1 reshape.12
  29.5 0.1 pad_add_fusion.1.info
  29.5 1.5 %collective-permute-done.4.sec1 = f32[2,64,256]{2,1,0:T(8,128)S(1)} collective-permute-done((f32[2,64,256]{2,1,0:T(8,128)S(1)}, f32[2,64,256]{2,1,0:T(8,128)S(1)}, u32[]{:S(2)}, u32[]{:S(2)}) %collective-permute-start.4) | collective-permute-done | bytes 131104 | tf_op jit(solution)/shard_map/ppermute | solution.py:242
  31.0 3.3 %collective-permute-done.5.sec2 = f32[2,64,256]{2,1,0:T(8,128)S(1)} collective-permute-done((f32[2,64,256]{2,1,0:T(8,128)S(1)}, f32[2,64,256]{2,1,0:T(8,128)S(1)}, u32[]{:S(2)}, u32[]{:S(2)}) %collective-permute-start.5) | collective-permute-done | bytes 131104 | tf_op jit(solution)/shard_map/ppermute | solution.py:242
  34.3 5.0 %collective-permute-done.6.sec3 = f32[2,64,256]{2,1,0:T(8,128)S(1)} collective-permute-done((f32[2,64,256]{2,1,0:T(8,128)S(1)}, f32[2,64,256]{2,1,0:T(8,128)S(1)}, u32[]{:S(2)}, u32[]{:S(2)}) %collective-permute-start.6) | collective-permute-done | bytes 131104 | tf_op jit(solution)/shard_map/ppermute | solution.py:242
  39.4 27.2 %shard_map.74 = f32[8,256]{1,0:T(8,128)S(1)} custom-call(s32[8]{0:T(128)S(1)} %pad_add_fusion.1.info, f32[2,3,96,32]{3,2,1,0:T(8,128)S(1)} %bitcast.16, f32[80,256]{1,0:T(8,128)S(1)} %get-tuple-element.8.feat, f32[2,8,256]{2,1,0:T(8,128)S(1)} %get-tuple-element.9.halo, f32[2,64,256]{2,1,0:T(8,128)S(1)} %get-tuple-element.10.sec0, ...), custom_call_target="tpu_custom_call" | custom-call | tf_op jit(solution)/shard_map/pallas_call | solution.py:296
  66.6 0.2 reshape.14
  66.8 0.2 copy.24
  67.0 0.7 %reshape.15 = f32[4,64]{1,0:T(4,128)} reshape(f32[4,8,8]{2,1,0:T(8,128)S(1)} %bitcast.20) | data formatting | bytes 2048 | tf_op jit(solution)/shard_map/reshape | solution.py:315
  (18 shorter events, 0.1 us)
Async XLA Ops:
  0.0 7.5 %copy-start.1 = (f32[4,64,256]{2,1,0:T(8,128)S(1)}, f32[4,64,256]{2,1,0:T(8,128)}, u32[]{:S(2)}) copy-start(f32[4,64,256]{2,1,0:T(8,128)} %ref.1) | copy-start | bytes 786436
  0.0 29.2 %collective-permute-start = (s32[2,1]{0,1:T(1,128)}, s32[2,1]{0,1:T(1,128)S(1)}, u32[]{:S(2)}, u32[]{:S(2)}) collective-permute-start(s32[2,1]{0,1:T(1,128)} %param.9), channel_id=1, source_target_pairs={{0,1},{1,2},{2,3},{3,4},{4,5},{5,6},{6,7},{7,8},{8,9},{9,10},{10,1... | collective-permute-start | bytes 32 | tf_op jit(solution)/shard_map/ppermute | solution.py:242
  4.7 24.6 %collective-permute-start.1 = (s32[2,1]{0,1:T(1,128)}, s32[2,1]{0,1:T(1,128)S(1)}, u32[]{:S(2)}, u32[]{:S(2)}) collective-permute-start(s32[2,1]{0,1:T(1,128)} %param.9), channel_id=1, source_target_pairs={{1,0},{2,1},{3,2},{4,3},{5,4},{6,5},{7,6},{8,7},{9,8},{10,9},{11,1... | collective-permute-start | bytes 32 | tf_op jit(solution)/shard_map/ppermute | solution.py:242
  7.5 5.7 %copy-start.2 = (f32[8,8,3,3,3]{1,0,4,3,2:T(8,128)S(1)}, f32[8,8,3,3,3]{1,0,4,3,2:T(8,128)}, u32[]{:S(2)}) copy-start(f32[8,8,3,3,3]{1,0,4,3,2:T(8,128)} %param.12) | copy-start | bytes 20740
  7.5 9.0 %collective-permute-start.2 = (f32[3,4,8,256]{3,2,1,0:T(8,128)S(1)}, f32[3,4,8,256]{3,2,1,0:T(8,128)S(1)}, u32[]{:S(2)}, u32[]{:S(2)}) collective-permute-start(f32[3,4,8,256]{3,2,1,0:T(8,128)S(1)} %pad_maximum_fusion.1), channel_id=1, source_target_pairs={{0,1},{1,2},{2,3},{3,4},{4,5},{5,6},{6,7},{7,8},{8,9},{9,10},{10,1... | collective-permute-start | bytes 294920 | tf_op jit(solution)/shard_map/ppermute | solution.py:242
  11.3 5.9 %collective-permute-start.3 = (f32[3,4,8,256]{3,2,1,0:T(8,128)S(1)}, f32[3,4,8,256]{3,2,1,0:T(8,128)S(1)}, u32[]{:S(2)}, u32[]{:S(2)}) collective-permute-start(f32[3,4,8,256]{3,2,1,0:T(8,128)S(1)} %pad_maximum_fusion.2), channel_id=1, source_target_pairs={{1,0},{2,1},{3,2},{4,3},{5,4},{6,5},{7,6},{8,7},{9,8},{10,9},{11,1... | collective-permute-start | bytes 294920 | tf_op jit(solution)/shard_map/ppermute | solution.py:242
  13.3 0.9 %copy-start.3 = (f32[8,8,3,3,3]{1,0,4,3,2:T(8,128)S(1)}, f32[8,8,3,3,3]{1,0,4,3,2:T(8,128)}, u32[]{:S(2)}) copy-start(f32[8,8,3,3,3]{1,0,4,3,2:T(8,128)} %param.13) | copy-start | bytes 20740
  14.3 0.8 %copy-start.4 = (f32[256,64]{0,1:T(8,128)S(1)}, f32[256,64]{0,1:T(8,128)}, u32[]{:S(2)}) copy-start(f32[256,64]{0,1:T(8,128)} %param.10) | copy-start | bytes 196612
  15.1 0.8 %copy-start.5 = (f32[256,64]{0,1:T(8,128)S(1)}, f32[256,64]{0,1:T(8,128)}, u32[]{:S(2)}) copy-start(f32[256,64]{0,1:T(8,128)} %param.11) | copy-start | bytes 196612
  16.2 1.1 %copy-start = (f32[2,4,64,256]{3,2,1,0:T(8,128)S(1)}, f32[2,4,64,256]{3,2,1,0:T(8,128)}, u32[]{:S(2)}) copy-start(f32[2,4,64,256]{3,2,1,0:T(8,128)} %sec.1) | copy-start | bytes 1572868
  24.7 4.6 %copy-start.6 = (s32[2,1]{0,1:T(1,128)S(1)}, s32[2,1]{0,1:T(1,128)}, u32[]{:S(2)}) copy-start(s32[2,1]{0,1:T(1,128)} %param.9) | copy-start | bytes 28
  24.7 6.3 %collective-permute-start.4 = (f32[2,64,256]{2,1,0:T(8,128)S(1)}, f32[2,64,256]{2,1,0:T(8,128)S(1)}, u32[]{:S(2)}, u32[]{:S(2)}) collective-permute-start(f32[2,64,256]{2,1,0:T(8,128)S(1)} %get-tuple-element.10.sec0), channel_id=1, source_target_pairs={{1,0},{2,1},{3,2},{4,3},{5,4},{6,5},{7,6},{8,7},{9,8},{10,9},{11,1... | collective-permute-start | bytes 393224 | tf_op jit(solution)/shard_map/ppermute | solution.py:242
  26.6 7.7 %collective-permute-start.5 = (f32[2,64,256]{2,1,0:T(8,128)S(1)}, f32[2,64,256]{2,1,0:T(8,128)S(1)}, u32[]{:S(2)}, u32[]{:S(2)}) collective-permute-start(f32[2,64,256]{2,1,0:T(8,128)S(1)} %get-tuple-element.10.sec0), channel_id=1, source_target_pairs={{2,0},{3,1},{4,2},{5,3},{6,4},{7,5},{8,6},{9,7},{10,8},{11,9},{12,... | collective-permute-start | bytes 393224 | tf_op jit(solution)/shard_map/ppermute | solution.py:242
  27.9 11.4 %collective-permute-start.6 = (f32[2,64,256]{2,1,0:T(8,128)S(1)}, f32[2,64,256]{2,1,0:T(8,128)S(1)}, u32[]{:S(2)}, u32[]{:S(2)}) collective-permute-start(f32[2,64,256]{2,1,0:T(8,128)S(1)} %get-tuple-element.10.sec0), channel_id=1, source_target_pairs={{3,0},{4,1},{5,2},{6,3},{7,4},{8,5},{9,6},{10,7},{11,8},{12,9},{13... | collective-permute-start | bytes 393224 | tf_op jit(solution)/shard_map/ppermute | solution.py:242

commit v2 on v1

v2 whole, which is shorter than its diff:
```python
import functools

import jax
import jax.numpy as jnp
from jax import lax
from jax.experimental import pallas as pl
from jax.experimental.pallas import tpu as pltpu
from jax.sharding import PartitionSpec as P

GROUPS = 8
DISP = 128
RAD = 3
ROWS = 4
CH = 64
LANES = ROWS * CH
HALO = 8
F32 = jnp.float32
BF16 = jnp.bfloat16


def dot(a, b):
    return jnp.dot(a, b, preferred_element_type=F32)


def split2(x):
    hi = x.astype(BF16)
    return hi, (x - hi.astype(F32)).astype(BF16)


def split3(x):
    hi = x.astype(BF16)
    rest = x - hi.astype(F32)
    mid = rest.astype(BF16)
    return hi, mid, (rest - mid.astype(F32)).astype(BF16)


def attend_kernel(images, width, count, offsets, ref, sec, wq, wv,
                  out_ref, out_sec, out_halo, next0, next1, next2, before, after,
                  left, right, stacked, edges, weights, query, value, scores, send, recv):
    wide = width + 2 * HALO
    tile = lax.axis_index("tile")
    nexts = (next0, next1, next2)

    def present(step):
        return (tile + step >= 0) & (tile + step < count)

    def remote(source, target, place, step):
        return pltpu.make_async_remote_copy(
            src_ref=source, dst_ref=target, send_sem=send.at[place], recv_sem=recv.at[place],
            device_id={"tile": tile + step}, device_id_type=pl.DeviceIdType.MESH)

    barrier = pltpu.get_barrier_semaphore()
    partners = 0
    for step in (1, -1, 2, -2, 3, -3):
        @pl.when(present(step))
        def _(step=step):
            pl.semaphore_signal(barrier, inc=1, device_id={"tile": tile + step}, device_id_type=pl.DeviceIdType.MESH)

        partners = partners + jnp.where(present(step), 1, 0)
    pl.semaphore_wait(barrier, partners)

    tail = pl.ds(width - HALO, HALO)
    head = pl.ds(0, HALO)
    upward = [
        remote(ref.at[:, tail, :], left.at[0], 0, 1),
        remote(sec.at[:, :, tail, :], left.at[pl.ds(1, images - 1)], 1, 1),
        remote(offsets, before, 2, 1),
    ]
    downward = [
        remote(ref.at[:, head, :], right.at[0], 3, -1),
        remote(sec.at[:, :, head, :], right.at[pl.ds(1, images - 1)], 4, -1),
        remote(offsets, after, 5, -1),
    ]
    for step, copies in ((1, upward), (-1, downward)):
        @pl.when(present(step))
        def _(copies=copies):
            for copy in copies:
                copy.start()
    for step, halo, entry in ((-1, left, before), (1, right, after)):
        @pl.when(jnp.logical_not(present(step)))
        def _(halo=halo, entry=entry):
            halo[...] = jnp.zeros_like(halo)
            entry[...] = jnp.zeros_like(entry)
    for step, buffer in ((1, next0), (2, next1), (3, next2)):
        @pl.when(jnp.logical_not(present(step)))
        def _(buffer=buffer):
            buffer[...] = jnp.zeros_like(buffer)

    weights[:, :CH] = wq[...]
    weights[:, CH:] = wv[...]
    zeros = jnp.zeros((HALO, LANES), F32)
    for image in range(images):
        for row in range(ROWS):
            stacked[row * width:(row + 1) * width, :] = ref[row] if image == 0 else sec[image - 1, row]
        both = jnp.dot(stacked[...], weights[...], precision=lax.Precision.HIGHEST, preferred_element_type=F32)
        for row in range(ROWS):
            part = both[row * width:(row + 1) * width, :]
            query[image, 2 * HALO:2 * HALO + width, row * CH:(row + 1) * CH] = part[:, :CH]
            value[image, 2 * HALO:2 * HALO + width, row * CH:(row + 1) * CH] = part[:, CH:]
        for buffer in (query, value):
            buffer[image, 0:HALO, :] = zeros
            buffer[image, HALO + wide:, :] = zeros
    for step, copies in ((1, upward), (-1, downward)):
        @pl.when(present(step))
        def _(copies=copies):
            for copy in copies:
                copy.wait_send()

        @pl.when(present(-step))
        def _(copies=copies):
            for copy in copies:
                copy.wait_recv()
    for image in range(images):
        for row in range(ROWS):
            base = (image * ROWS + row) * 2 * HALO
            edges[base:base + HALO, :] = left[image, row]
            edges[base + HALO:base + 2 * HALO, :] = right[image, row]
    both = jnp.dot(edges[...], weights[...], precision=lax.Precision.HIGHEST, preferred_element_type=F32)
    for image in range(images):
        for row in range(ROWS):
            base = (image * ROWS + row) * 2 * HALO
            lanes = slice(row * CH, (row + 1) * CH)
            query[image, HALO:2 * HALO, lanes] = both[base:base + HALO, :CH]
            value[image, HALO:2 * HALO, lanes] = both[base:base + HALO, CH:]
            query[image, HALO + wide - HALO:HALO + wide, lanes] = both[base + HALO:base + 2 * HALO, :CH]
            value[image, HALO + wide - HALO:HALO + wide, lanes] = both[base + HALO:base + 2 * HALO, CH:]
    ones = jnp.where(
        lax.broadcasted_iota(jnp.int32, (LANES, LANES), 0) // CH
        == lax.broadcasted_iota(jnp.int32, (LANES, LANES), 1) // CH,
        1.0 / CH, 0.0).astype(BF16)

    def attention(image, length):
        lane_row = lax.broadcasted_iota(jnp.int32, (length, LANES), 1) // CH
        column = lax.broadcasted_iota(jnp.int32, (length, LANES), 0) + (tile * width - HALO)
        own = query[image, HALO:HALO + length, :]
        peak = jnp.full((length, LANES), -1e30, F32)
        place = 0
        for shift in range(-RAD, RAD + 1):
            keys = query[image, HALO + shift:HALO + shift + length, :]
            col_ok = (column + shift >= 0) & (column + shift < count * width)
            for step in (-1, 0, 1):
                moved = pltpu.roll(keys, (-step * CH) % LANES, 1) if step else keys
                hi, mid, low = split3(own * moved)
                score = dot(hi, ones) + dot(mid, ones) + dot(low, ones)
                row_ok = (lane_row + step >= 0) & (lane_row + step < ROWS)
                score = jnp.where(col_ok & row_ok, score, -1e30)
                scores[place, :length] = score
                peak = jnp.maximum(peak, score)
                place += 1
        total = jnp.zeros((length, LANES), F32)
        mixed = jnp.zeros((length, LANES), F32)
        place = 0
        for shift in range(-RAD, RAD + 1):
            vals = value[image, HALO + shift:HALO + shift + length, :]
            for step in (-1, 0, 1):
                moved = pltpu.roll(vals, (-step * CH) % LANES, 1) if step else vals
                weight = jnp.exp(scores[place, :length] - peak)
                total = total + weight
                mixed = mixed + weight * moved
                place += 1
        return column, value[image, HALO:HALO + length, :] + mixed / total

    sends = []
    for pair in range(images - 1):
        _, feature = attention(pair + 1, HALO + width)
        out_halo[pair] = feature[:HALO]
        out_sec[pair] = feature[HALO:]
        for step in (1, 2, 3):
            copy = remote(out_sec.at[pair], nexts[step - 1].at[pair], 6 + 3 * pair + step - 1, -step)
            sends.append((step, copy))

            @pl.when(present(-step))
            def _(copy=copy):
                copy.start()

    column, feature = attention(0, wide)
    out_ref[...] = jnp.where((column >= 0) & (column < count * width), feature, 0.0)
    for step, copy in sends:
        @pl.when(present(-step))
        def _(copy=copy):
            copy.wait_send()

        @pl.when(present(step))
        def _(copy=copy):
            copy.wait_recv()


def cost_kernel(pairs, width, info, taps, feat, halo, sec0, sec1, sec2, sec3, out,
                window, moved, padded, prod, plane, high, low, tail_high, tail_low, w_high, w_low, wt_high, wt_low, means):
    group = ROWS * GROUPS
    blocks = width // 8
    block = 8 * group
    edge_span = 2 * group
    full = (width + 4) * group
    tail = blocks * block
    tiles = DISP + 16
    window[...] = jnp.zeros_like(window)
    for pair in range(pairs):
        window[pair, 0:HALO, :] = halo[pair]
        for place, sec in enumerate((sec0, sec1, sec2, sec3)):
            window[pair, HALO + place * width:HALO + (place + 1) * width, :] = sec[pair]
        plane[pair, 0:8, :] = jnp.zeros((8, full), F32)
        plane[pair, 8 + DISP:, :] = jnp.zeros((8, full), F32)
    padded[...] = jnp.zeros_like(padded)
    padded[0:width + 2 * HALO, :] = feat[...]
    for conv in range(2):
        wt_high[conv] = jnp.zeros((block, block), BF16)
        wt_low[conv] = jnp.zeros((block, block), BF16)
        for tap in range(3):
            w_high[conv, tap] = jnp.zeros((block, block), BF16)
            w_low[conv, tap] = jnp.zeros((block, block), BF16)
            hi, lo = split2(taps[conv, tap])
            for col in range(8):
                lanes = slice(col * group, (col + 1) * group)
                inside = min(3, 8 - col) * group
                w_high[conv, tap, col * group:col * group + inside, lanes] = hi[:inside]
                w_low[conv, tap, col * group:col * group + inside, lanes] = lo[:inside]
                if inside < 3 * group:
                    base = tap * edge_span
                    wt_high[conv, base:base + 3 * group - inside, lanes] = hi[inside:]
                    wt_low[conv, base:base + 3 * group - inside, lanes] = lo[inside:]
    feat_hi, feat_lo = split2(padded[...].T)
    lane = lax.broadcasted_iota(jnp.int32, (DISP, 128), 1)

    def left_matrix(at):
        rows = lax.broadcasted_iota(jnp.int32, (128, block), 0)
        lanes = lax.broadcasted_iota(jnp.int32, (128, block), 1)
        spread = jnp.where(rows == lanes // group + (8 * at + HALO - 2), 1.0, 0.0).astype(BF16)
        keep = jnp.where(
            lax.broadcasted_iota(jnp.int32, (LANES, block), 0) // GROUPS
            == lax.broadcasted_iota(jnp.int32, (LANES, block), 1) % group,
            1.0 / (CH // GROUPS), 0.0)
        return (dot(feat_hi, spread) * keep).astype(BF16), (dot(feat_lo, spread) * keep).astype(BF16)

    def shifted(pair, offset, start, count):
        first = offset + (HALO - 2)
        rest = first % 8
        aligned = pl.multiple_of(first - rest + start, 8)
        rows = window[pair, pl.ds(aligned, count + 8), :]
        return pltpu.roll(rows, count + 8 - rest, 0)[:count]

    def skewed(rows, left_hi, left_lo, halves):
        right_hi, right_lo = split2(rows)
        prod[...] = dot(right_hi, left_hi) + dot(right_hi, left_lo) + dot(right_lo, left_hi)
        result = []
        for half in range(halves):
            lanes = slice(half * 128, (half + 1) * 128)
            value = prod[half * 4:half * 4 + DISP, lanes]
            for col in range(1, 4):
                other = prod[half * 4 + col:half * 4 + col + DISP, lanes]
                value = jnp.where(lane >= col * group, other, value)
            result.append(value)
        return result

    for pair in range(pairs):
        moved[pair] = shifted(pair, info[3 * pair], 0, width + tiles)

    def volume_step(at, carry):
        left_hi, left_lo = left_matrix(at)
        for pair in range(pairs):
            parts = skewed(moved[pair, pl.ds(pl.multiple_of(8 * at, 8), tiles), :], left_hi, left_lo, 2)
            for half in range(2):
                plane[pair, 8:8 + DISP, pl.ds(pl.multiple_of(at * block + half * 128, 128), 128)] = parts[half]
        return carry

    lax.fori_loop(0, blocks, volume_step, 0)
    left_hi, left_lo = left_matrix(0)
    for pair in range(pairs):
        (edge,) = skewed(shifted(pair, info[3 * pair + 1], 0, tiles), left_hi, left_lo, 1)
        plane[pair, 8:8 + DISP, 0:128] = jnp.where(lane < 2 * group, edge, plane[pair, 8:8 + DISP, 0:128])
    left_hi, left_lo = left_matrix(blocks)
    for pair in range(pairs):
        (mine,) = skewed(moved[pair, width:width + tiles, :], left_hi, left_lo, 1)
        (edge,) = skewed(shifted(pair, info[3 * pair + 2], width, tiles), left_hi, left_lo, 1)
        plane[pair, 8:8 + DISP, tail:tail + 128] = jnp.where(lane < 2 * group, mine, edge)

    def split_chunk(at, with_tail):
        lanes = pl.ds(pl.multiple_of(at * 128, 128), 128)
        for pair in range(pairs):
            rows = slice(pair * DISP, (pair + 1) * DISP)
            parts = [plane[pair, 7 + tap:7 + tap + DISP, lanes] for tap in range(3)]
            for tap in range(3):
                hi, lo = split2(parts[tap])
                high[tap, rows, lanes] = hi
                low[tap, rows, lanes] = lo
            if with_tail:
                base = pl.multiple_of(at * 128 - block, 128)
                mix = jnp.where(lane < edge_span, parts[0], pltpu.roll(parts[1], edge_span, 1))
                for place, part in ((0, split2(mix)), (128, (hi, lo))):
                    to = pl.ds(pl.multiple_of(base + place, 128), 128)
                    tail_high[rows, to] = part[0]
                    tail_low[rows, to] = part[1]

    def split_planes():
        split_chunk(0, False)
        split_chunk(1, False)

        def step(at, carry):
            split_chunk(2 * at, True)
            split_chunk(2 * at + 1, False)
            return carry

        lax.fori_loop(1, blocks, step, 0)
        split_chunk(2 * blocks, True)

    def conv(which, start):
        lanes = pl.ds(start, block)
        edge_hi = tail_high[:, lanes]
        total = dot(edge_hi, wt_high[which]) + dot(edge_hi, wt_low[which]) + dot(tail_low[:, lanes], wt_high[which])
        for tap in range(3):
            hi = high[tap, :, lanes]
            total = total + dot(hi, w_high[which, tap])
            total = total + dot(hi, w_low[which, tap])
            total = total + dot(low[tap, :, lanes], w_high[which, tap])
        return jnp.maximum(total, 0.0)

    def conv_end(which, start):
        lanes = pl.ds(start, 128)
        total = None
        for tap in range(3):
            hi = high[tap, :, lanes]
            wh = w_high[which, tap, 0:128, 0:128]
            wl = w_low[which, tap, 0:128, 0:128]
            term = dot(hi, wh) + dot(hi, wl) + dot(low[tap, :, lanes], wh)
            total = term if total is None else total + term
        return jnp.maximum(total, 0.0)

    split_planes()
    is_first, is_last = info[3 * pairs], info[3 * pairs + 1]

    def first_step(at, carry):
        start = pl.multiple_of(at * block, block)
        result = conv(0, start)
        lanes = lax.broadcasted_iota(jnp.int32, result.shape, 1)
        result = jnp.where((lanes < group) & (is_first + jnp.where(at == 0, 1, 0) == 2), 0.0, result)
        for pair in range(pairs):
            plane[pair, 8:8 + DISP, pl.ds(start, block)] = result[pair * DISP:(pair + 1) * DISP]
        return carry

    lax.fori_loop(0, blocks, first_step, 0)
    result = conv_end(0, tail)
    lanes = lax.broadcasted_iota(jnp.int32, result.shape, 1)
    result = jnp.where((lanes >= group) & (is_last == 1), 0.0, result)
    for pair in range(pairs):
        plane[pair, 8:8 + DISP, tail:tail + 128] = result[pair * DISP:(pair + 1) * DISP]
    split_planes()
    level = lax.broadcasted_iota(jnp.int32, (DISP, block), 0).astype(F32)

    def second_step(at, carry):
        result = conv(1, pl.multiple_of(at * block, block))
        score = result[:DISP]
        for pair in range(1, pairs):
            score = score + result[pair * DISP:(pair + 1) * DISP]
        for shift in (4, 2, 1):
            score = score + pltpu.roll(score, block - shift, 1)
        weight = jnp.exp(score - jnp.max(score, axis=0, keepdims=True))
        mean = jnp.sum(weight * level, axis=0, keepdims=True) / jnp.sum(weight, axis=0, keepdims=True)
        means[pl.ds(at, 1), :] = mean / DISP
        return carry

    lax.fori_loop(0, blocks, second_step, 0)
    own_row = lax.broadcasted_iota(jnp.int32, (8, block), 0) * GROUPS
    own_row = own_row == lax.broadcasted_iota(jnp.int32, (8, block), 1) % group
    from_lane = lax.broadcasted_iota(jnp.int32, (block, width), 0) // group
    to_col = lax.broadcasted_iota(jnp.int32, (block, width), 1)
    total = jnp.zeros((8, width), F32)
    for at in range(blocks):
        pick = jnp.where(from_lane + 8 * at == to_col, 1.0, 0.0).astype(BF16)
        for part in split3(jnp.where(own_row, jnp.broadcast_to(means[at:at + 1, :], (8, block)), 0.0)):
            total = total + dot(part, pick)
    out[...] = total[:ROWS]


def exchange(pairs, width, count, features):
    images = pairs + 1
    wide = width + 2 * HALO
    vmem = pl.BlockSpec(memory_space=pltpu.VMEM)
    shifted = jax.ShapeDtypeStruct((pairs, width, LANES), F32)
    entry = jax.ShapeDtypeStruct((pairs, 128), jnp.int32)
    copies = 6 + 3 * pairs

    def ordered(*args):
        feat, own, halo, next0, next1, next2, before, after = call(*args)
        return feat, halo, own, next0, next1, next2, before, after

    call = pl.pallas_call(
        functools.partial(attend_kernel, images, width, count),
        out_shape=(
            jax.ShapeDtypeStruct((wide, LANES), F32),
            shifted,
            jax.ShapeDtypeStruct((pairs, HALO, LANES), F32),
            shifted, shifted, shifted, entry, entry,
        ),
        in_specs=[vmem] * 5,
        out_specs=(vmem,) * 8,
        scratch_shapes=[
            pltpu.VMEM((images, ROWS, HALO, features), F32),
            pltpu.VMEM((images, ROWS, HALO, features), F32),
            pltpu.VMEM((ROWS * width, features), F32),
            pltpu.VMEM((images * ROWS * 2 * HALO, features), F32),
            pltpu.VMEM((features, 2 * CH), F32),
            pltpu.VMEM((images, wide + 2 * HALO, LANES), F32),
            pltpu.VMEM((images, wide + 2 * HALO, LANES), F32),
            pltpu.VMEM((3 * (2 * RAD + 1), wide, LANES), F32),
            pltpu.SemaphoreType.DMA((copies,)),
            pltpu.SemaphoreType.DMA((copies,)),
        ],
        compiler_params=pltpu.CompilerParams(
            vmem_limit_bytes=24 << 20, collective_id=0, has_side_effects=True),
    )
    return ordered


def tap_matrices(conv_first, conv_second):
    both = jnp.stack([conv_first, conv_second])
    flipped = jnp.transpose(both, (0, 5, 4, 3, 2, 1))
    rows = jnp.pad(flipped, ((0, 0), (0, 0), (0, 0), (ROWS - 1, ROWS - 1), (0, 0), (0, 0)))
    parts = [rows[:, :, :, ROWS - out:2 * ROWS - out] for out in range(ROWS)]
    joined = jnp.concatenate(parts, axis=-1)
    return joined.reshape(2, 3, 3 * ROWS * GROUPS, ROWS * GROUPS)


def on_device(reference_feat, secondary_feat, pair_offsets, w_query_key, w_value, conv_first, conv_second):
    pairs = secondary_feat.shape[0]
    width = reference_feat.shape[1]
    tile_id = lax.axis_index("tile")
    count = lax.axis_size("tile")
    group = ROWS * GROUPS
    full = (width + 4) * group
    vmem = pl.BlockSpec(memory_space=pltpu.VMEM)
    smem = pl.BlockSpec(memory_space=pltpu.SMEM)
    features = reference_feat.shape[2]
    entries = jnp.broadcast_to(pair_offsets, (pairs, 128))
    taps = tap_matrices(conv_first, conv_second)
    feat, halo, own, next0, next1, next2, before, after = exchange(
        pairs, width, lax.axis_size("tile"), features)(entries, reference_feat, secondary_feat, w_query_key, w_value)
    info = jnp.concatenate([
        jnp.concatenate([pair_offsets, before[:, :1], after[:, :1]], axis=1).reshape(-1),
        jnp.stack([tile_id == 0, tile_id == count - 1]).astype(jnp.int32),
    ])
    return pl.pallas_call(
        functools.partial(cost_kernel, pairs, width),
        out_shape=jax.ShapeDtypeStruct((ROWS, width), F32),
        in_specs=[smem] + [vmem] * 7,
        out_specs=vmem,
        scratch_shapes=[
            pltpu.VMEM((pairs, HALO + 4 * width + 16, LANES), F32),
            pltpu.VMEM((pairs, width + DISP + 16, LANES), F32),
            pltpu.VMEM((128, LANES), F32),
            pltpu.VMEM((DISP + 16, 8 * group), F32),
            pltpu.VMEM((pairs, DISP + 16, full), F32),
            pltpu.VMEM((3, pairs * DISP, full), BF16),
            pltpu.VMEM((3, pairs * DISP, full), BF16),
            pltpu.VMEM((pairs * DISP, width * group), BF16),
            pltpu.VMEM((pairs * DISP, width * group), BF16),
            pltpu.VMEM((2, 3, 8 * group, 8 * group), BF16),
            pltpu.VMEM((2, 3, 8 * group, 8 * group), BF16),
            pltpu.VMEM((2, 8 * group, 8 * group), BF16),
            pltpu.VMEM((2, 8 * group, 8 * group), BF16),
            pltpu.VMEM((width // 8, 8 * group), F32),
        ],
        compiler_params=pltpu.CompilerParams(vmem_limit_bytes=48 << 20),
    )(info, taps, feat, halo, own, next0, next1, next2)


def solution(mesh):
    return jax.shard_map(
        on_device,
        mesh=mesh,
        in_specs=(
            P("groups", "tile", None),
            P("groups", None, "tile", None),
            P("groups", "tile"),
            P(),
            P(),
            P(),
            P(),
        ),
        out_specs=P("groups", "tile"),
        check_vma=False,
    )
```

time: 68.2 us -> 51 us (0.75)
  starting transfers between devices: 16.8 us -> 0 us
  Pallas kernels: 34.6 us -> 46.3 us
  waiting for transfers between devices: 10.6 us -> 0 us
  local copies, waits for them, and re-layouts: 4.93 us -> 3.89 us
    ppermute x7 -> x0, starting transfers between devices: 16.8 us -> none  [passed_along(): lax.ppermute(value, axis, [(source, source + steps) for source in range(f...]
    pallas_call x1, Pallas kernels: 7.41 us -> 18.8 us  [ordered(): feat, own, halo, next0, next1, next2, before, after = call(*args)]
    ppermute x7 -> x0, waiting for transfers between devices: 10.6 us -> none  [passed_along(): lax.ppermute(value, axis, [(source, source + steps) for source in range(f...]
    slice x1 -> x0, local copies, waits for them, and re-layouts: 0.88 us -> none  [on_device(): secondary_feat[:, :, :HALO]]
    reshape x3 -> x1, local copies, waits for them, and re-layouts: 0.96 us -> 0.08 us  [on_device(): jnp.concatenate([pair_offsets, before[:, :1], after[:, :1]], axis=1)]
    unnamed x19 -> x17, local copies, waits for them, and re-layouts: 2.89 us -> 3.64 us
  transfers between devices with their start and end apart: 7 -> 0, of which waited for: 4 -> 0; matrix products, arithmetic and copies ran while one was open for 3% -> 0% of each run, Pallas kernels for 11% -> 0%
where the time goes in v2:
time: 51 us; the launch traced here: 50.9 us
  Pallas kernels  46.3 us (91%)
  local copies, waits for them, and re-layouts  3.89 us (8%)
  other arithmetic  0.54 us (1%)
    pallas_call x1, Pallas kernels, on_device(): pl.pallas_call(functools.partial(cost_kernel, pairs, width), out_shape=ja...  27.6 us
    pallas_call x1, Pallas kernels, ordered(): feat, own, halo, next0, next1, next2, before, after = call(*args)  18.8 us
    unnamed x17, local copies, waits for them, and re-layouts  3.64 us

profile of v2, /device:TPU:1, one launch (start us, length us, event | category | flops | bytes accessed | tf_op | source)
XLA Modules:
  0.0 50.9 jit_solution(3684397686659881961)
XLA Ops:
  0.0 0.1 add_convert_fusion
  0.1 0.0 copy-start.5
  0.1 0.7 %copy-done.5 = s32[2,1]{0,1:T(1,128)S(1)} copy-done((s32[2,1]{0,1:T(1,128)S(1)}, s32[2,1]{0,1:T(1,128)}, u32[]{:S(2)}) %copy-start.5) | copy-done | bytes 32
  0.7 0.1 broadcast_in_dim.8.offsets
  0.8 0.1 copy.14
  0.9 0.0 copy-start.2
  0.9 1.0 %copy.15 = f32[8,8,3,3,3]{0,1,2,3,4:T(8,128)S(1)} copy(f32[8,8,3,3,3]{1,0,4,3,2:T(8,128)} %param.12) | data formatting | bytes 13824 | tf_op args[5]
  1.9 0.0 copy-done.2
  1.9 0.0 copy-start
  1.9 0.1 copy.16
  2.0 0.0 copy-start.3
  2.0 0.0 copy-start.4
  2.1 0.8 %copy-done.3 = f32[256,64]{0,1:T(8,128)S(1)} copy-done((f32[256,64]{0,1:T(8,128)S(1)}, f32[256,64]{0,1:T(8,128)}, u32[]{:S(2)}) %copy-start.3) | copy-done | bytes 65560
  2.9 0.0 copy-start.1
  2.9 0.1 copy.12.wq
  3.0 0.0 copy-done.4
  3.0 0.1 copy.13.wv
  3.1 0.0 copy-done
  3.1 0.7 %copy-done.1 = f32[4,64,256]{2,1,0:T(8,128)S(1)} copy-done((f32[4,64,256]{2,1,0:T(8,128)S(1)}, f32[4,64,256]{2,1,0:T(8,128)}, u32[]{:S(2)}) %copy-start.1) | copy-done | bytes 262168
  3.9 18.8 %shard_map.73 = (f32[80,256]{1,0:T(8,128)S(1)}, f32[2,64,256]{2,1,0:T(8,128)S(1)}, f32[2,8,256]{2,1,0:T(8,128)S(1)}, f32[2,64,256]{2,1,0:T(8,128)S(1)}, f32[2,64...) custom-call(s32[2,128]{1,0:T(2,128)S(1)} %broadcast_in_dim.8.offsets, ...), custom_call_target="tpu_custom_call" | custom-call | tf_op jit(solution)/shard_map/pallas_call | solution.py:383
  22.7 0.1 pad_add_fusion
  22.7 0.1 reshape.6
  22.8 0.1 pad_add_fusion.1.info
  22.9 0.1 pad_slice_fusion.3
  23.0 0.3 pad_maximum_fusion
  23.3 27.6 %shard_map.74 = f32[4,64]{1,0:T(4,128)} custom-call(s32[8]{0:T(128)S(1)} %pad_add_fusion.1.info, f32[2,3,96,32]{3,2,1,0:T(8,128)S(1)} %bitcast.10, f32[80,256]{1,0:T(8,128)S(1)} %get-tuple-element.15.feat, f32[2,8,256]{2,1,0:T(8,128)S(1)} %get-tuple-element.16.halo, f32[2,64,256]{2,1,0:T(8,128)S(1)} %get-tuple-element.17.sec0, ...), custom_call_target="tpu_custom_call" | custom-call | tf_op jit(solution)/shard_map/pallas_call | solution.py:441
  (1 shorter events, 0.0 us)
Async XLA Ops:
  0.1 0.7 %copy-start.5 = (s32[2,1]{0,1:T(1,128)S(1)}, s32[2,1]{0,1:T(1,128)}, u32[]{:S(2)}) copy-start(s32[2,1]{0,1:T(1,128)} %param.9) | copy-start | bytes 28
  0.9 1.0 %copy-start.2 = (f32[8,8,3,3,3]{1,0,4,3,2:T(8,128)S(1)}, f32[8,8,3,3,3]{1,0,4,3,2:T(8,128)}, u32[]{:S(2)}) copy-start(f32[8,8,3,3,3]{1,0,4,3,2:T(8,128)} %param.13) | copy-start | bytes 20740
  1.9 1.2 %copy-start = (f32[2,4,64,256]{3,2,1,0:T(8,128)S(1)}, f32[2,4,64,256]{3,2,1,0:T(8,128)}, u32[]{:S(2)}) copy-start(f32[2,4,64,256]{3,2,1,0:T(8,128)} %sec.1) | copy-start | bytes 1572868
  2.0 0.9 %copy-start.3 = (f32[256,64]{0,1:T(8,128)S(1)}, f32[256,64]{0,1:T(8,128)}, u32[]{:S(2)}) copy-start(f32[256,64]{0,1:T(8,128)} %param.10) | copy-start | bytes 196612
  2.0 1.0 %copy-start.4 = (f32[256,64]{0,1:T(8,128)S(1)}, f32[256,64]{0,1:T(8,128)}, u32[]{:S(2)}) copy-start(f32[256,64]{0,1:T(8,128)} %param.11) | copy-start | bytes 196612
  2.9 1.0 %copy-start.1 = (f32[4,64,256]{2,1,0:T(8,128)S(1)}, f32[4,64,256]{2,1,0:T(8,128)}, u32[]{:S(2)}) copy-start(f32[4,64,256]{2,1,0:T(8,128)} %ref.1) | copy-start | bytes 786436

commit v3 on v2

--- a/solution.py
+++ b/solution.py
@@ -1,4 +1,5 @@
 import functools
+from functools import reduce
 
 import jax
 import jax.numpy as jnp
@@ -22,6 +23,10 @@
     return jnp.dot(a, b, preferred_element_type=F32)
 
 
+def aligned(start):
+    return start if isinstance(start, int) else pl.multiple_of(start, 128)
+
+
 def split2(x):
     hi = x.astype(BF16)
     return hi, (x - hi.astype(F32)).astype(BF16)
@@ -51,7 +56,7 @@
 
     barrier = pltpu.get_barrier_semaphore()
     partners = 0
-    for step in (1, -1, 2, -2, 3, -3):
+    for step in (1, -1, 3, -3):
         @pl.when(present(step))
         def _(step=step):
             pl.semaphore_signal(barrier, inc=1, device_id={"tile": tile + step}, device_id_type=pl.DeviceIdType.MESH)
@@ -165,7 +170,7 @@
         _, feature = attention(pair + 1, HALO + width)
         out_halo[pair] = feature[:HALO]
         out_sec[pair] = feature[HALO:]
-        for step in (1, 2, 3):
+        for step in (1, 3):
             copy = remote(out_sec.at[pair], nexts[step - 1].at[pair], 6 + 3 * pair + step - 1, -step)
             sends.append((step, copy))
 
@@ -175,68 +180,91 @@
 
     column, feature = attention(0, wide)
     out_ref[...] = jnp.where((column >= 0) & (column < count * width), feature, 0.0)
+    odd = tile % 2 == 1
+    forwards = []
+    for step, copy in sends:
+        @pl.when(present(step))
+        def _(copy=copy):
+            copy.wait_recv()
+
+        pair = len(forwards) // 2
+        source, offset, chosen = (next0, -1, odd) if step == 1 else (next2, 1, jnp.logical_not(odd))
+        forward = remote(source.at[pair], next1.at[pair], 7 + 3 * pair, offset)
+        going = chosen & present(step)
+        forwards.append((going, forward))
+
+        @pl.when(going)
+        def _(forward=forward):
+            forward.start()
+
     for step, copy in sends:
         @pl.when(present(-step))
         def _(copy=copy):
             copy.wait_send()
 
-        @pl.when(present(step))
-        def _(copy=copy):
-            copy.wait_recv()
+    for going, forward in forwards:
+        @pl.when(going)
+        def _(forward=forward):
+            forward.wait_send()
+
+    for _, forward in forwards[::2]:
+        @pl.when(present(2))
+        def _(forward=forward):
+            forward.wait_recv()
 
 
 def cost_kernel(pairs, width, info, taps, feat, halo, sec0, sec1, sec2, sec3, out,
-                window, moved, padded, prod, plane, high, low, tail_high, tail_low, w_high, w_low, wt_high, wt_low, means):
+                window, moved, padded, prod, keep, gap, side, high, low, ends, w_high, w_low, w_ends, means):
     group = ROWS * GROUPS
     blocks = width // 8
     block = 8 * group
     edge_span = 2 * group
-    full = (width + 4) * group
     tail = blocks * block
     tiles = DISP + 16
-    window[...] = jnp.zeros_like(window)
+    window[:, HALO + 4 * width:, :] = jnp.zeros((pairs, 16, LANES), F32)
     for pair in range(pairs):
         window[pair, 0:HALO, :] = halo[pair]
         for place, sec in enumerate((sec0, sec1, sec2, sec3)):
             window[pair, HALO + place * width:HALO + (place + 1) * width, :] = sec[pair]
-        plane[pair, 0:8, :] = jnp.zeros((8, full), F32)
-        plane[pair, 8 + DISP:, :] = jnp.zeros((8, full), F32)
+        for place in range(2):
+            side[place, pair, 0:8, :] = jnp.zeros((8, block), F32)
+            side[place, pair, 8 + DISP:, :] = jnp.zeros((8, block), F32)
     padded[...] = jnp.zeros_like(padded)
     padded[0:width + 2 * HALO, :] = feat[...]
     for conv in range(2):
-        wt_high[conv] = jnp.zeros((block, block), BF16)
-        wt_low[conv] = jnp.zeros((block, block), BF16)
         for tap in range(3):
             w_high[conv, tap] = jnp.zeros((block, block), BF16)
             w_low[conv, tap] = jnp.zeros((block, block), BF16)
+            w_ends[conv, tap] = jnp.zeros((block, block), BF16)
             hi, lo = split2(taps[conv, tap])
             for col in range(8):
                 lanes = slice(col * group, (col + 1) * group)
                 inside = min(3, 8 - col) * group
+                rest = 3 * group - inside
                 w_high[conv, tap, col * group:col * group + inside, lanes] = hi[:inside]
                 w_low[conv, tap, col * group:col * group + inside, lanes] = lo[:inside]
-                if inside < 3 * group:
-                    base = tap * edge_span
-                    wt_high[conv, base:base + 3 * group - inside, lanes] = hi[inside:]
-                    wt_low[conv, base:base + 3 * group - inside, lanes] = lo[inside:]
+                if rest:
+                    w_ends[conv, tap, 0:rest, lanes] = hi[inside:]
+                    w_ends[conv, tap, edge_span:edge_span + rest, lanes] = hi[inside:]
+                    w_ends[conv, tap, 2 * edge_span:2 * edge_span + rest, lanes] = lo[inside:]
+    lanes = lax.broadcasted_iota(jnp.int32, (128, block), 1)
+    gap[...] = lax.broadcasted_iota(jnp.int32, (128, block), 0) - (lanes >> 5)
+    keep[...] = jnp.where(
+        lax.broadcasted_iota(jnp.int32, (LANES, block), 0) >> 3
+        == (lax.broadcasted_iota(jnp.int32, (LANES, block), 1) & (group - 1)),
+        1.0 / (CH // GROUPS), 0.0)
     feat_hi, feat_lo = split2(padded[...].T)
     lane = lax.broadcasted_iota(jnp.int32, (DISP, 128), 1)
 
     def left_matrix(at):
-        rows = lax.broadcasted_iota(jnp.int32, (128, block), 0)
-        lanes = lax.broadcasted_iota(jnp.int32, (128, block), 1)
-        spread = jnp.where(rows == lanes // group + (8 * at + HALO - 2), 1.0, 0.0).astype(BF16)
-        keep = jnp.where(
-            lax.broadcasted_iota(jnp.int32, (LANES, block), 0) // GROUPS
-            == lax.broadcasted_iota(jnp.int32, (LANES, block), 1) % group,
-            1.0 / (CH // GROUPS), 0.0)
-        return (dot(feat_hi, spread) * keep).astype(BF16), (dot(feat_lo, spread) * keep).astype(BF16)
+        spread = jnp.where(gap[...] == 8 * at + (HALO - 2), 1.0, 0.0).astype(BF16)
+        return (dot(feat_hi, spread) * keep[...]).astype(BF16), (dot(feat_lo, spread) * keep[...]).astype(BF16)
 
     def shifted(pair, offset, start, count):
         first = offset + (HALO - 2)
         rest = first % 8
-        aligned = pl.multiple_of(first - rest + start, 8)
-        rows = window[pair, pl.ds(aligned, count + 8), :]
+        base = pl.multiple_of(first - rest + start, 8)
+        rows = window[pair, pl.ds(base, count + 8), :]
         return pltpu.roll(rows, count + 8 - rest, 0)[:count]
 
     def skewed(rows, left_hi, left_lo, halves):
@@ -255,102 +283,92 @@
     for pair in range(pairs):
         moved[pair] = shifted(pair, info[3 * pair], 0, width + tiles)
 
+    def keep_first(pair, at, value):
+        rows = slice(pair * DISP, (pair + 1) * DISP)
+        start = at * block
+        hi, lo = split2(value)
+        mix = jnp.where(lane < edge_span, hi.astype(F32), pltpu.roll(lo.astype(F32), edge_span, 1))
+        high[rows, pl.ds(aligned(start), 128)] = hi
+        low[rows, pl.ds(aligned(start), 128)] = lo
+        ends[rows, pl.ds(aligned(start), 128)] = mix.astype(BF16)
+        ends[rows, pl.ds(aligned(start + 128), 128)] = hi
+
+    def keep_second(pair, at, value):
+        rows = slice(pair * DISP, (pair + 1) * DISP)
+        hi, lo = split2(value)
+        high[rows, pl.ds(aligned(at * block + 128), 128)] = hi
+        low[rows, pl.ds(aligned(at * block + 128), 128)] = lo
+
     def volume_step(at, carry):
         left_hi, left_lo = left_matrix(at)
         for pair in range(pairs):
             parts = skewed(moved[pair, pl.ds(pl.multiple_of(8 * at, 8), tiles), :], left_hi, left_lo, 2)
-            for half in range(2):
-                plane[pair, 8:8 + DISP, pl.ds(pl.multiple_of(at * block + half * 128, 128), 128)] = parts[half]
+            keep_first(pair, at, parts[0])
+            keep_second(pair, at, parts[1])
         return carry
 
-    lax.fori_loop(0, blocks, volume_step, 0)
+    lax.fori_loop(1, blocks, volume_step, 0)
     left_hi, left_lo = left_matrix(0)
     for pair in range(pairs):
+        mine, second = skewed(moved[pair, 0:tiles, :], left_hi, left_lo, 2)
         (edge,) = skewed(shifted(pair, info[3 * pair + 1], 0, tiles), left_hi, left_lo, 1)
-        plane[pair, 8:8 + DISP, 0:128] = jnp.where(lane < 2 * group, edge, plane[pair, 8:8 + DISP, 0:128])
+        keep_first(pair, 0, jnp.where(lane < 2 * group, edge, mine))
+        keep_second(pair, 0, second)
     left_hi, left_lo = left_matrix(blocks)
     for pair in range(pairs):
         (mine,) = skewed(moved[pair, width:width + tiles, :], left_hi, left_lo, 1)
         (edge,) = skewed(shifted(pair, info[3 * pair + 2], width, tiles), left_hi, left_lo, 1)
-        plane[pair, 8:8 + DISP, tail:tail + 128] = jnp.where(lane < 2 * group, mine, edge)
-
-    def split_chunk(at, with_tail):
-        lanes = pl.ds(pl.multiple_of(at * 128, 128), 128)
+        keep_first(pair, blocks, jnp.where(lane < 2 * group, mine, edge))
+
+    def joined(products, count):
+        for place in range(2):
+            for pair in range(pairs):
+                side[place, pair, 8:8 + DISP, 0:count] = products[2 * place][pair * DISP:(pair + 1) * DISP]
+        return [
+            jnp.maximum(
+                side[0, pair, 7:7 + DISP, 0:count] + products[1][pair * DISP:(pair + 1) * DISP]
+                + side[1, pair, 9:9 + DISP, 0:count], 0.0)
+            for pair in range(pairs)
+        ]
+
+    def conv(which, at):
+        hi = high[:, pl.ds(aligned(at * block), block)]
+        lo = low[:, pl.ds(aligned(at * block), block)]
+        end = ends[:, pl.ds(aligned(at * block + block), block)]
+        return joined([
+            dot(hi, w_high[which, tap]) + dot(hi, w_low[which, tap])
+            + dot(lo, w_high[which, tap]) + dot(end, w_ends[which, tap])
+            for tap in range(3)
+        ], block)
+
+    def conv_end(which):
+        hi = high[:, tail:tail + 128]
+        lo = low[:, tail:tail + 128]
+        return joined([
+            dot(hi, w_high[which, tap, 0:128, 0:128]) + dot(hi, w_low[which, tap, 0:128, 0:128])
+            + dot(lo, w_high[which, tap, 0:128, 0:128])
+            for tap in range(3)
+        ], 128)
+
+    is_first, is_last = info[3 * pairs], info[3 * pairs + 1]
+
+    def first_step(at, carry):
+        results = conv(0, at)
         for pair in range(pairs):
-            rows = slice(pair * DISP, (pair + 1) * DISP)
-            parts = [plane[pair, 7 + tap:7 + tap + DISP, lanes] for tap in range(3)]
-            for tap in range(3):
-                hi, lo = split2(parts[tap])
-                high[tap, rows, lanes] = hi
-                low[tap, rows, lanes] = lo
-            if with_tail:
-                base = pl.multiple_of(at * 128 - block, 128)
-                mix = jnp.where(lane < edge_span, parts[0], pltpu.roll(parts[1], edge_span, 1))
-                for place, part in ((0, split2(mix)), (128, (hi, lo))):
-                    to = pl.ds(pl.multiple_of(base + place, 128), 128)
-                    tail_high[rows, to] = part[0]
-                    tail_low[rows, to] = part[1]
-
-    def split_planes():
-        split_chunk(0, False)
-        split_chunk(1, False)
-
-        def step(at, carry):
-            split_chunk(2 * at, True)
-            split_chunk(2 * at + 1, False)
-            return carry
-
-        lax.fori_loop(1, blocks, step, 0)
-        split_chunk(2 * blocks, True)
-
-    def conv(which, start):
-        lanes = pl.ds(start, block)
-        edge_hi = tail_high[:, lanes]
-        total = dot(edge_hi, wt_high[which]) + dot(edge_hi, wt_low[which]) + dot(tail_low[:, lanes], wt_high[which])
-        for tap in range(3):
-            hi = high[tap, :, lanes]
-            total = total + dot(hi, w_high[which, tap])
-            total = total + dot(hi, w_low[which, tap])
-            total = total + dot(low[tap, :, lanes], w_high[which, tap])
-        return jnp.maximum(total, 0.0)
-
-    def conv_end(which, start):
-        lanes = pl.ds(start, 128)
-        total = None
-        for tap in range(3):
-            hi = high[tap, :, lanes]
-            wh = w_high[which, tap, 0:128, 0:128]
-            wl = w_low[which, tap, 0:128, 0:128]
-            term = dot(hi, wh) + dot(hi, wl) + dot(low[tap, :, lanes], wh)
-            total = term if total is None else total + term
-        return jnp.maximum(total, 0.0)
-
-    split_planes()
-    is_first, is_last = info[3 * pairs], info[3 * pairs + 1]
-
-    def first_step(at, carry):
-        start = pl.multiple_of(at * block, block)
-        result = conv(0, start)
-        lanes = lax.broadcasted_iota(jnp.int32, result.shape, 1)
-        result = jnp.where((lanes < group) & (is_first + jnp.where(at == 0, 1, 0) == 2), 0.0, result)
-        for pair in range(pairs):
-            plane[pair, 8:8 + DISP, pl.ds(start, block)] = result[pair * DISP:(pair + 1) * DISP]
+            first = results[pair][:, :128]
+            outside = is_first + jnp.where(at == 0, 1, 0) == 2
+            keep_first(pair, at, jnp.where((lane < group) & outside, 0.0, first))
+            keep_second(pair, at, results[pair][:, 128:])
         return carry
 
     lax.fori_loop(0, blocks, first_step, 0)
-    result = conv_end(0, tail)
-    lanes = lax.broadcasted_iota(jnp.int32, result.shape, 1)
-    result = jnp.where((lanes >= group) & (is_last == 1), 0.0, result)
+    results = conv_end(0)
     for pair in range(pairs):
-        plane[pair, 8:8 + DISP, tail:tail + 128] = result[pair * DISP:(pair + 1) * DISP]
-    split_planes()
+        keep_first(pair, blocks, jnp.where((lane >= group) & (is_last == 1), 0.0, results[pair]))
     level = lax.broadcasted_iota(jnp.int32, (DISP, block), 0).astype(F32)
 
     def second_step(at, carry):
-        result = conv(1, pl.multiple_of(at * block, block))
-        score = result[:DISP]
-        for pair in range(1, pairs):
-            score = score + result[pair * DISP:(pair + 1) * DISP]
+        score = reduce(jnp.add, conv(1, at))
         for shift in (4, 2, 1):
             score = score + pltpu.roll(score, block - shift, 1)
         weight = jnp.exp(score - jnp.max(score, axis=0, keepdims=True))
@@ -426,7 +444,7 @@
     tile_id = lax.axis_index("tile")
     count = lax.axis_size("tile")
     group = ROWS * GROUPS
-    full = (width + 4) * group
+    full = (width + 8) * group
     vmem = pl.BlockSpec(memory_space=pltpu.VMEM)
     smem = pl.BlockSpec(memory_space=pltpu.SMEM)
     features = reference_feat.shape[2]
@@ -448,15 +466,15 @@
             pltpu.VMEM((pairs, width + DISP + 16, LANES), F32),
             pltpu.VMEM((128, LANES), F32),
             pltpu.VMEM((DISP + 16, 8 * group), F32),
-            pltpu.VMEM((pairs, DISP + 16, full), F32),
-            pltpu.VMEM((3, pairs * DISP, full), BF16),
-            pltpu.VMEM((3, pairs * DISP, full), BF16),
-            pltpu.VMEM((pairs * DISP, width * group), BF16),
-            pltpu.VMEM((pairs * DISP, width * group), BF16),
+            pltpu.VMEM((LANES, 8 * group), F32),
+            pltpu.VMEM((128, 8 * group), jnp.int32),
+            pltpu.VMEM((2, pairs, DISP + 16, 8 * group), F32),
+            pltpu.VMEM((pairs * DISP, full), BF16),
+            pltpu.VMEM((pairs * DISP, full), BF16),
+            pltpu.VMEM((pairs * DISP, full), BF16),
             pltpu.VMEM((2, 3, 8 * group, 8 * group), BF16),
             pltpu.VMEM((2, 3, 8 * group, 8 * group), BF16),
-            pltpu.VMEM((2, 8 * group, 8 * group), BF16),
-            pltpu.VMEM((2, 8 * group, 8 * group), BF16),
+            pltpu.VMEM((2, 3, 8 * group, 8 * group), BF16),
             pltpu.VMEM((width // 8, 8 * group), F32),
         ],
         compiler_params=pltpu.CompilerParams(vmem_limit_bytes=48 << 20),

time: 51 us -> 45 us (0.88)
  Pallas kernels: 46.3 us -> 40.3 us
    pallas_call x1, Pallas kernels: 27.6 us -> 24.2 us  [on_device(): pl.pallas_call(functools.partial(cost_kernel, pairs, width), out_shape=ja...]
    pallas_call x1, Pallas kernels: 18.8 us -> 16 us  [ordered(): feat, own, halo, next0, next1, next2, before, after = call(*args)]
where the time goes in v3:
time: 45 us; the launch traced here: 44.8 us
  Pallas kernels  40.3 us (90%)
  local copies, waits for them, and re-layouts  3.89 us (9%)
  other arithmetic  0.54 us (1%)
    pallas_call x1, Pallas kernels, on_device(): pl.pallas_call(functools.partial(cost_kernel, pairs, width), out_shape=ja...  24.2 us
    pallas_call x1, Pallas kernels, ordered(): feat, own, halo, next0, next1, next2, before, after = call(*args)  16 us
    unnamed x17, local copies, waits for them, and re-layouts  3.64 us

profile of v3, /device:TPU:1, one launch (start us, length us, event | category | flops | bytes accessed | tf_op | source)
XLA Modules:
  0.0 44.8 jit_solution(7701366506878734808)
XLA Ops:
  0.0 0.1 add_convert_fusion
  0.1 0.0 copy-start.5
  0.1 0.7 %copy-done.5 = s32[2,1]{0,1:T(1,128)S(1)} copy-done((s32[2,1]{0,1:T(1,128)S(1)}, s32[2,1]{0,1:T(1,128)}, u32[]{:S(2)}) %copy-start.5) | copy-done | bytes 32
  0.7 0.1 broadcast_in_dim.8.offsets
  0.8 0.1 copy.14
  0.9 0.0 copy-start.2
  0.9 1.0 %copy.15 = f32[8,8,3,3,3]{0,1,2,3,4:T(8,128)S(1)} copy(f32[8,8,3,3,3]{1,0,4,3,2:T(8,128)} %param.12) | data formatting | bytes 13824 | tf_op args[5]
  1.9 0.0 copy-done.2
  1.9 0.0 copy-start
  1.9 0.1 copy.16
  2.0 0.0 copy-start.3
  2.0 0.0 copy-start.4
  2.1 0.8 %copy-done.3 = f32[256,64]{0,1:T(8,128)S(1)} copy-done((f32[256,64]{0,1:T(8,128)S(1)}, f32[256,64]{0,1:T(8,128)}, u32[]{:S(2)}) %copy-start.3) | copy-done | bytes 65560
  2.9 0.0 copy-start.1
  2.9 0.1 copy.12.wq
  3.0 0.0 copy-done.4
  3.0 0.1 copy.13.wv
  3.1 0.0 copy-done
  3.1 0.7 %copy-done.1 = f32[4,64,256]{2,1,0:T(8,128)S(1)} copy-done((f32[4,64,256]{2,1,0:T(8,128)S(1)}, f32[4,64,256]{2,1,0:T(8,128)}, u32[]{:S(2)}) %copy-start.1) | copy-done | bytes 262168
  3.9 16.0 %shard_map.73 = (f32[80,256]{1,0:T(8,128)S(1)}, f32[2,64,256]{2,1,0:T(8,128)S(1)}, f32[2,8,256]{2,1,0:T(8,128)S(1)}, f32[2,64,256]{2,1,0:T(8,128)S(1)}, f32[2,64...) custom-call(s32[2,128]{1,0:T(2,128)S(1)} %broadcast_in_dim.8.offsets, ...), custom_call_target="tpu_custom_call" | custom-call | tf_op jit(solution)/shard_map/pallas_call | solution.py:401
  19.9 0.1 pad_add_fusion
  20.0 0.1 reshape.6
  20.1 0.1 pad_add_fusion.1.info
  20.2 0.1 pad_slice_fusion.3
  20.3 0.3 pad_maximum_fusion
  20.6 24.2 %shard_map.74 = f32[4,64]{1,0:T(4,128)} custom-call(s32[8]{0:T(128)S(1)} %pad_add_fusion.1.info, f32[2,3,96,32]{3,2,1,0:T(8,128)S(1)} %bitcast.10, f32[80,256]{1,0:T(8,128)S(1)} %get-tuple-element.15.feat, f32[2,8,256]{2,1,0:T(8,128)S(1)} %get-tuple-element.16.halo, f32[2,64,256]{2,1,0:T(8,128)S(1)} %get-tuple-element.17.sec0, ...), custom_call_target="tpu_custom_call" | custom-call | tf_op jit(solution)/shard_map/pallas_call | solution.py:459
  (1 shorter events, 0.0 us)
Async XLA Ops:
  0.1 0.7 %copy-start.5 = (s32[2,1]{0,1:T(1,128)S(1)}, s32[2,1]{0,1:T(1,128)}, u32[]{:S(2)}) copy-start(s32[2,1]{0,1:T(1,128)} %param.9) | copy-start | bytes 28
  0.9 1.0 %copy-start.2 = (f32[8,8,3,3,3]{1,0,4,3,2:T(8,128)S(1)}, f32[8,8,3,3,3]{1,0,4,3,2:T(8,128)}, u32[]{:S(2)}) copy-start(f32[8,8,3,3,3]{1,0,4,3,2:T(8,128)} %param.13) | copy-start | bytes 20740
  1.9 1.2 %copy-start = (f32[2,4,64,256]{3,2,1,0:T(8,128)S(1)}, f32[2,4,64,256]{3,2,1,0:T(8,128)}, u32[]{:S(2)}) copy-start(f32[2,4,64,256]{3,2,1,0:T(8,128)} %sec.1) | copy-start | bytes 1572868
  2.0 0.9 %copy-start.3 = (f32[256,64]{0,1:T(8,128)S(1)}, f32[256,64]{0,1:T(8,128)}, u32[]{:S(2)}) copy-start(f32[256,64]{0,1:T(8,128)} %param.10) | copy-start | bytes 196612
  2.0 1.0 %copy-start.4 = (f32[256,64]{0,1:T(8,128)S(1)}, f32[256,64]{0,1:T(8,128)}, u32[]{:S(2)}) copy-start(f32[256,64]{0,1:T(8,128)} %param.11) | copy-start | bytes 196612
  2.9 1.0 %copy-start.1 = (f32[4,64,256]{2,1,0:T(8,128)S(1)}, f32[4,64,256]{2,1,0:T(8,128)}, u32[]{:S(2)}) copy-start(f32[4,64,256]{2,1,0:T(8,128)} %ref.1) | copy-start | bytes 786436
